TPU v7x, 256 devices: a whole 4x4x8 slice. The times are simulated.
256 devices in a mesh: grp: 8 (over z), blk: 32 (over y, x, core).
Axes of the slice: x: 4, y: 4, z: 8, core: 2. Of those that a mesh axis runs over, the one named last changes fastest.
Arguments:
- inputs: bfloat16 [65536, 128], P(('grp', 'blk')), may hold values from -6 to 6
- targets: bfloat16 [65536], P(('grp', 'blk')), may hold values from -6 to 6
- weight_in: float32 [128, 512], replicated, may hold values from -0.5 to 0.5
- bias_in: float32 [512], replicated, may hold values from -3 to 3
- weight_out: float32 [512, 128], replicated, may hold values from -0.25 to 0.25
- neighbors: int32 [512, 2], replicated, may hold values from 0 to 511, as said below
- owner_map: int32 [512], replicated, may hold values from 0 to 511, as said below
Outputs:
- whitened: float32 [65536], P(('grp', 'blk'))
- trained_in: float32 [128, 512], replicated
- trained_bias: float32 [512], replicated
- trained_out: float32 [512, 128], replicated
Inputs may be any that keep to these rules, and one draw needn't show every extreme that they name: A permutation of the block ids: block i is stored at position owner_map[i], which lies on device owner_map[i] // 2 in the grp+blk order. `neighbors`: row p holds the ids of the 2 conditioning blocks of the block at position p: distinct, stored on devices of the same grp index other than the block's own device. Of the 4 conditioning blocks of one device's blocks, at most 1 lie on any one device, and every device takes exactly 1 from some device. In every grp index one block conditions a block on every other device of that grp index.
All inputs are finite; a program needn't handle non-finite values.
Results may differ from a plain program's by a relative error of at most 0.0025.
Values may be sent and summed in bfloat16 or wider, within the bound.
A program may use at most 64 MiB of HBM per device.

v0:
```python
import jax
import jax.numpy as jnp
from jax import lax
from jax.sharding import PartitionSpec as P

PTS = 128
FEAT = 128
M = 2


nugget = 0.5
step_length = 3.0
epsilon = 1e-06
highest = lax.Precision.HIGHEST


def silu_slope(preact):
    logistic = jax.nn.sigmoid(preact)
    return logistic * (1.0 + preact * (1.0 - logistic))


def features_of(rows_in, weight_in16, bias_now, weight_out16):
    preact = jnp.dot(rows_in, weight_in16, preferred_element_type=jnp.float32) + bias_now
    hidden = jax.nn.silu(preact).astype(jnp.bfloat16)
    features = jnp.dot(hidden, weight_out16, preferred_element_type=jnp.float32).astype(
        jnp.bfloat16
    )
    return (preact, hidden, features)


def mlp_backward(rows_in, preact, hidden, cotangent, weight_out16):
    grad_out = jnp.dot(hidden.astype(jnp.float32).T, cotangent, precision=highest)
    backed = jnp.dot(cotangent, weight_out16.astype(jnp.float32).T, precision=highest) * silu_slope(
        preact
    )
    grad_in = jnp.dot(rows_in.astype(jnp.float32).T, backed, precision=highest)
    return (grad_in, jnp.sum(backed, axis=0), grad_out)


def lower_solve(factor_mat, right_side, flipped):
    return lax.linalg.triangular_solve(
        factor_mat, right_side, left_side=True, lower=True, transpose_a=flipped
    )


def kernel_block(left_rows, right_rows, left_sq, right_sq):
    cross_term = jnp.einsum(
        "bpf,bqf->bpq", left_rows, right_rows, preferred_element_type=jnp.float32
    )
    distance = left_sq[:, :, None] + right_sq[:, None, :] - 2.0 * cross_term
    return jnp.exp(distance * (-2.0 / left_rows.shape[2]))


def swap_last(matrix):
    return jnp.swapaxes(matrix, 1, 2)


def block_terms(feat_b, feat_c, target_b, target_c, weight):
    wide_b = feat_b.astype(jnp.float32)
    wide_c = feat_c.astype(jnp.float32)
    sq_b = jnp.sum(wide_b * wide_b, axis=2)
    sq_c = jnp.sum(wide_c * wide_c, axis=2)
    exp_cc = kernel_block(feat_c, feat_c, sq_c, sq_c)
    exp_cb = kernel_block(feat_c, feat_b, sq_c, sq_b)
    exp_bb = kernel_block(feat_b, feat_b, sq_b, sq_b)
    eye_c = jnp.eye(feat_c.shape[1], dtype=jnp.float32)
    eye_b = jnp.eye(feat_b.shape[1], dtype=jnp.float32)
    chol_c = jnp.linalg.cholesky(exp_cc + nugget * eye_c)
    projected = lower_solve(chol_c, exp_cb, False)
    white_c = lower_solve(chol_c, target_c.astype(jnp.float32)[:, :, None], False)
    schur_part = (
        exp_bb
        + nugget * eye_b
        - jnp.einsum("bcp,bcq->bpq", projected, projected, precision=highest)
    )
    chol_s = jnp.linalg.cholesky(schur_part)
    residual = target_b.astype(jnp.float32)[:, :, None] - jnp.einsum(
        "bcp,bcz->bpz", projected, white_c, precision=highest
    )
    whitened = lower_solve(chol_s, residual, False)
    solved = lower_solve(chol_c, projected, True)
    coef_c = lower_solve(chol_c, white_c, True)
    coef_b = lower_solve(chol_s, whitened, True)
    inv_s = lower_solve(chol_s, jnp.broadcast_to(eye_b, chol_s.shape), False)
    half_p = 0.5 * (
        jnp.einsum("bqp,bqr->bpr", inv_s, inv_s, precision=highest) - coef_b * swap_last(coef_b)
    )
    w_half = jnp.einsum("bcp,bpq->bcq", solved, half_p, precision=highest)
    w_beta = jnp.einsum("bcp,bpz->bcz", solved, coef_b, precision=highest)
    grad_cb = -2.0 * w_half - coef_c * swap_last(coef_b)
    grad_cc = jnp.einsum("bcp,bdp->bcd", w_half, solved, precision=highest) + 0.5 * (
        w_beta * swap_last(coef_c) + coef_c * swap_last(w_beta)
    )
    e_cc = grad_cc * exp_cc
    e_cb = 0.5 * grad_cb * exp_cb
    e_bb = half_p * exp_bb
    factor = -8.0 * weight / feat_b.shape[2]
    cot_c = factor * (
        (jnp.sum(e_cc, axis=2) + jnp.sum(e_cb, axis=2))[:, :, None] * wide_c
        - jnp.einsum("bcd,bdf->bcf", e_cc, wide_c, precision=highest)
        - jnp.einsum("bcp,bpf->bcf", e_cb, wide_b, precision=highest)
    )
    cot_b = factor * (
        (jnp.sum(e_cb, axis=1) + jnp.sum(e_bb, axis=2))[:, :, None] * wide_b
        - jnp.einsum("bcp,bcf->bpf", e_cb, wide_c, precision=highest)
        - jnp.einsum("bpq,bqf->bpf", e_bb, wide_b, precision=highest)
    )
    return (whitened[:, :, 0], cot_b, cot_c)


def apply_update(params, gradients):
    totals = lax.psum((gradients[0], gradients[1], gradients[2]), ("grp", "blk"))
    squares = (
        jnp.sum(totals[0] * totals[0])
        + jnp.sum(totals[1] * totals[1])
        + jnp.sum(totals[2] * totals[2])
    )
    scaling = step_length / jnp.sqrt(squares + epsilon)
    return (
        params[0] - scaling * totals[0],
        params[1] - scaling * totals[1],
        params[2] - scaling * totals[2],
    )


def shards(inputs, targets, weight_in, bias_in, weight_out, neighbors, owner_map):
    peer_count = lax.axis_size("blk")
    my_index = lax.axis_index("blk")
    region = lax.axis_index("grp")
    blocks = inputs.shape[0] // PTS
    requests = blocks * M
    capacity = (requests + peer_count - 2) // (peer_count - 1)
    region_rows = peer_count * blocks
    region_ids = lax.dynamic_slice_in_dim(neighbors, region * region_rows, region_rows, 0)
    region_pos = jnp.take(owner_map, region_ids.reshape(-1), axis=0).reshape(peer_count, requests)
    owner_peer = region_pos // blocks % peer_count
    owner_local = region_pos % blocks
    request_ids = jnp.arange(requests)
    earlier = request_ids[:, None] < request_ids[None, :]
    same_owner = owner_peer[:, :, None] == owner_peer[:, None, :]
    slot_rank = jnp.sum(jnp.logical_and(same_owner, earlier[None]).astype(jnp.int32), axis=1)
    slot_ids = jnp.arange(capacity)
    local_ids = jnp.arange(blocks)
    picked = (
        (owner_peer == my_index)[:, :, None, None]
        & (slot_rank[:, :, None, None] == slot_ids[None, None, :, None])
        & (owner_local[:, :, None, None] == local_ids[None, None, None, :])
    )
    select16 = jnp.sum(picked.astype(jnp.float32), axis=1).astype(jnp.bfloat16)
    my_peer = lax.dynamic_index_in_dim(owner_peer, my_index, 0, keepdims=False)
    my_rank = lax.dynamic_index_in_dim(slot_rank, my_index, 0, keepdims=False)
    my_slot = my_peer * capacity + my_rank
    placing = (
        (my_peer[:, None, None] == jnp.arange(peer_count)[None, :, None])
        & (my_rank[:, None, None] == slot_ids[None, None, :])
    ).astype(jnp.bfloat16)
    target_blocks = targets.reshape(blocks, PTS)
    weight = 1.0 / neighbors.shape[0]
    params = (weight_in, bias_in, weight_out)
    weight_in16 = params[0].astype(jnp.bfloat16)
    weight_out16 = params[2].astype(jnp.bfloat16)
    preact, hidden, features = features_of(inputs, weight_in16, params[1], weight_out16)
    feat_own = features.reshape(blocks, PTS, FEAT)
    send_targets = jnp.einsum(
        "rsk,kp->rsp", select16, target_blocks, preferred_element_type=jnp.float32
    ).astype(jnp.bfloat16)
    send_rows = jnp.einsum(
        "rsk,kpf->rspf", select16, feat_own, preferred_element_type=jnp.float32
    ).astype(jnp.bfloat16)
    got_rows = lax.all_to_all(send_rows, "blk", split_axis=0, concat_axis=0, tiled=True)
    got_targets = lax.all_to_all(send_targets, "blk", split_axis=0, concat_axis=0, tiled=True)
    feat_c = jnp.take(got_rows.reshape(peer_count * capacity, PTS, FEAT), my_slot, axis=0).reshape(
        blocks, M * PTS, FEAT
    )
    target_c = jnp.take(got_targets.reshape(peer_count * capacity, PTS), my_slot, axis=0).reshape(
        blocks, M * PTS
    )
    whitened, cot_b, cot_c = block_terms(feat_own, feat_c, target_blocks, target_c, weight)
    use_cots = cot_c.reshape(requests, PTS, FEAT).astype(jnp.bfloat16)
    back_rows = jnp.einsum(
        "irs,ipf->rspf", placing, use_cots, preferred_element_type=jnp.float32
    ).astype(jnp.bfloat16)
    got_back = lax.all_to_all(back_rows, "blk", split_axis=0, concat_axis=0, tiled=True)
    total_cot = cot_b + jnp.einsum(
        "rsk,rspf->kpf", select16, got_back, preferred_element_type=jnp.float32
    )
    gradients = mlp_backward(inputs, preact, hidden, total_cot.reshape(-1, FEAT), weight_out16)
    params = apply_update(params, gradients)
    return (whitened.reshape(-1), params[0], params[1], params[2])


def solution(mesh):
    placed = (P(("grp", "blk"), None), P(("grp", "blk")), P(), P(), P(), P(), P())
    return jax.shard_map(
        shards,
        mesh=mesh,
        in_specs=placed,
        out_specs=(P(("grp", "blk")), P(), P(), P()),
        check_vma=False,
    )
```

profile of v0, /device:TPU:1, one launch (start us, length us, event | category | flops | bytes accessed | tf_op | source)
XLA Modules:
  0.0 516.4 jit_solution(7676465352173806750)
XLA Ops:
  7.2 0.8 constant_dynamic-slice_fusion.1
  8.3 1.6 gather_fusion
  10.4 0.8 fusion.12
  11.8 8.6 %all-to-all-start.1 = ((bf16[32,1,128]{2,1,0:T(2,128)(2,1)}), bf16[32,1,128]{2,1,0:T(2,128)(2,1)S(1)}, u32[]{:S(2)}, u32[]{:S(2)}) async-start(bf16[32,1,128]{2,1,0:T(2,128)(2,1)} %copy.175), calls=%async_computation.1 | async-start | bytes 32768 | tf_op jit(solution)/shard_map/all_to_all | solution.py:171
  20.8 2.0 multiply_convert_fusion
  24.4 1.4 copy.163
  26.1 1.3 all-to-all-done.1
  27.3 6.2 %all-to-all-start = ((bf16[32,1,128,128]{3,2,1,0:T(8,128)(2,1)}), bf16[32,1,128,128]{3,2,1,0:T(8,128)(2,1)S(1)}, u32[]{:S(2)}, u32[]{:S(2)}) async-start(bf16[32,1,128,128]{3,2,1,0:T(8,128)(2,1)} %copy.163), calls=%async_computation | async-start | bytes 2097152 | tf_op jit(solution)/shard_map/all_to_all | solution.py:170
  35.9 14.6 %all-to-all-done = bf16[32,1,128,128]{3,2,1,0:T(8,128)(2,1)S(1)} async-done(((bf16[32,1,128,128]{3,2,1,0:T(8,128)(2,1)}), bf16[32,1,128,128]{3,2,1,0:T(8,128)(2,1)S(1)}, u32[]{:S(2)}, u32[]{:S(2)}) %all-to-all-start) | async-done | bytes 1048608 | tf_op jit(solution)/shard_map/all_to_all | solution.py:170
  51.7 0.9 fusion.6
  53.3 23.5 %custom-call.33 = f32[2,128,128]{2,1,0:T(8,128)S(1)} custom-call(f32[2,128,128]{2,1,0:T(8,128)S(1)} %cholesky.138), custom_call_target="Cholesky" | custom-call | tf_op jit(solution)/shard_map/jit(cholesky)/cholesky | solution.py:68
  76.8 19.7 %custom-call.34 = f32[2,1,128,128]{2,3,1,0:T(8,128)S(1)} custom-call(f32[2,1,128,128]{3,2,1,0:T(8,128)S(1)} %select_bitcast_fusion.1), custom_call_target="InvertDiagBlocksLowerTriangular" | custom-call | tf_op jit(solution)/shard_map/jit(cholesky)/cholesky | solution.py:68
  97.2 23.5 %custom-call.35 = f32[2,128,128]{2,1,0:T(8,128)S(1)} custom-call(f32[2,128,128]{2,1,0:T(8,128)S(1)} %convolution_subtract_fusion.6), custom_call_target="Cholesky" | custom-call | tf_op jit(solution)/shard_map/jit(cholesky)/cholesky | solution.py:68
  121.2 5.4 %while.1 = (s32[]{:T(128)}, f32[2,256,256]{2,1,0:T(8,128)S(1)}, s32[2,2]{1,0:T(2,128)S(1)}, f32[2,2,128,128]{3,2,0,1:T(8,128)}, s32[]{:T(128)}) while((s32[]{:T(128)}, f32[2,256,256]{2,1,0:T(8,128)S(1)}, s32[2,2]{1,0:T(2,128)S(1)}, f32[2,2,128,128]{3,2,0,1:T(8,128)}, s32[]{:T(128)}) %tuple.50), condition=%wide.while_cond, body=%wide.while_body.sunk | while | flops 2 | bytes 263777 | solution.py:41
  121.8 2.0 bitcast_dynamic-update-slice_fusion.2
  124.5 2.0 bitcast_dynamic-update-slice_fusion.2
  126.5 40.1 %custom-call.36 = f32[2,2,128,128]{2,3,1,0:T(8,128)S(1)} custom-call(f32[2,2,128,128]{3,2,1,0:T(8,128)} %bitcast.225), custom_call_target="InvertDiagBlocksLowerTriangular" | custom-call | tf_op jit(solution)/shard_map/triangular_solve | solution.py:41
  171.5 23.5 %custom-call.37 = f32[2,128,128]{2,1,0:T(8,128)S(1)} custom-call(f32[2,128,128]{2,1,0:T(8,128)S(1)} %fusion.33), custom_call_target="Cholesky" | custom-call | tf_op jit(solution)/shard_map/jit(cholesky)/cholesky | solution.py:76
  195.0 0.8 select_reduce_fusion
  196.0 19.9 %custom-call.38 = f32[2,1,128,128]{2,3,1,0:T(8,128)S(1)} custom-call(f32[2,1,128,128]{3,2,1,0:T(8,128)S(1)} %select_bitcast_fusion), custom_call_target="InvertDiagBlocksLowerTriangular" | custom-call | tf_op jit(solution)/shard_map/triangular_solve | solution.py:41
  218.5 0.8 fusion.89
  220.6 1.4 copy.183
  222.0 4.1 all-to-all-start.2
  226.4 16.9 %all-to-all-done.2 = bf16[32,1,128,128]{3,2,1,0:T(8,128)(2,1)S(1)} async-done(((bf16[32,1,128,128]{3,2,1,0:T(8,128)(2,1)}), bf16[32,1,128,128]{3,2,1,0:T(8,128)(2,1)S(1)}, u32[]{:S(2)}, u32[]{:S(2)}) %all-to-all-start.2) | async-done | bytes 1048608 | tf_op jit(solution)/shard_map/all_to_all | solution.py:183
  244.4 1.2 fusion.91
  246.0 1.3 convolution_bitcast_fusion
  247.5 78.5 %psum.22 = f32[512]{0:T(512)S(1)} all-reduce(f32[512]{0:T(512)S(1)} %get-tuple-element.78), channel_id=1, replica_groups=mesh['grp'=8,'blk'=32] {'grp','blk'}, use_global_device_ids=true, to_apply=%region_17.18 | all-reduce | flops 512 | bytes 4096 | tf_op jit(solution)/shard_map/psum | solution.py:112
  326.7 174.4 %all-reduce.4.cloned.1.call-done = (f32[128,512]{0,1:T(8,128)}, f32[512,128]{1,0:T(8,128)}) async-done(((f32[128,512]{0,1:T(8,128)}, f32[512,128]{1,0:T(8,128)}), (f32[128,512]{0,1:T(8,128)}, f32[512,128]{1,0:T(8,128)})) %all-reduce.4.cloned.1.call-update) | async-done | bytes 524304 | tf_op jit(solution)/shard_map/psum | solution.py:112
  501.0 1.7 multiply_reduce_fusion.1
  502.7 1.6 multiply_reduce_fusion
  506.4 1.7 multiply_subtract_fusion
  508.7 0.8 copy.187
  (167 shorter events, 22.2 us)
Async XLA Ops:
  7.2 13.6 %copy-start = (bf16[256,128]{1,0:T(8,128)(2,1)S(1)}, bf16[256,128]{1,0:T(8,128)(2,1)}, u32[]{:S(2)}) copy-start(bf16[256,128]{1,0:T(8,128)(2,1)} %param.7) | copy-start | bytes 196612
  10.4 13.2 %copy-start.16 = (bf16[32,2]{0,1:T(2,128)(2,1)}, bf16[32,2]{0,1:T(2,128)(2,1)S(1)}, u32[]{:S(2)}) copy-start(bf16[32,2]{0,1:T(2,128)(2,1)S(1)} %convert_reduce_fusion.1) | copy-start | bytes 388
  11.8 15.5 %all-to-all-start.1 = ((bf16[32,1,128]{2,1,0:T(2,128)(2,1)}), bf16[32,1,128]{2,1,0:T(2,128)(2,1)S(1)}, u32[]{:S(2)}, u32[]{:S(2)}) async-start(bf16[32,1,128]{2,1,0:T(2,128)(2,1)} %copy.175), calls=%async_computation.1 | async-start | bytes 32768 | tf_op jit(solution)/shard_map/all_to_all | solution.py:171
  20.7 14.1 %copy-start.18 = (s32[4]{0:T(128)}, s32[4]{0:T(128)S(1)}, u32[]{:S(2)}) copy-start(s32[4]{0:T(128)S(1)} %get-tuple-element.42) | copy-start | bytes 52
  20.8 99.8 %copy-start.9 = (pred[128,128]{1,0:T(8,128)(4,1)}, pred[128,128]{1,0:T(8,128)(4,1)S(1)}, u32[]{:S(2)}) copy-start(pred[128,128]{1,0:T(8,128)(4,1)S(1)} %iota_compare_fusion.4) | copy-start | bytes 49156
  20.8 2.0 copy-start.3
  22.9 0.7 copy-start.1
  27.3 23.2 %all-to-all-start = ((bf16[32,1,128,128]{3,2,1,0:T(8,128)(2,1)}), bf16[32,1,128,128]{3,2,1,0:T(8,128)(2,1)S(1)}, u32[]{:S(2)}, u32[]{:S(2)}) async-start(bf16[32,1,128,128]{3,2,1,0:T(8,128)(2,1)} %copy.163), calls=%async_computation | async-start | bytes 2097152 | tf_op jit(solution)/shard_map/all_to_all | solution.py:170
  35.9 15.8 %copy-start.21 = (bf16[2,256,1]{1,0,2:T(2,128)(2,1)}, bf16[2,256,1]{1,0,2:T(2,128)(2,1)S(1)}, u32[]{:S(2)}) copy-start(bf16[2,256,1]{1,0,2:T(2,128)(2,1)S(1)} %broadcast_select_fusion) | copy-start | bytes 3076
  96.8 24.3 %copy-start.26 = (s32[2]{0:T(128)S(1)}, s32[2]{0:T(128)}, u32[]{:S(2)}) copy-start(s32[2]{0:T(128)} %iota_multiply_fusion) | copy-start | bytes 28
  120.9 45.7 %copy-start.5 = (f32[2,256,128]{2,1,0:T(8,128)S(1)}, f32[2,256,128]{2,1,0:T(8,128)}, u32[]{:S(2)}) copy-start(f32[2,256,128]{2,1,0:T(8,128)} %fusion.6) | copy-start | bytes 786436
  167.4 2.0 slice-start
  167.8 2.1 copy-start.22
  169.6 1.1 copy-start.10
  170.1 0.6 copy-start.14
  170.7 45.5 %copy-start.24 = (bf16[256]{0:T(256)(128)(2,1)S(1)}, bf16[256]{0:T(256)(128)(2,1)}, u32[]{:S(2)}) copy-start(bf16[256]{0:T(256)(128)(2,1)} %param.8) | copy-start | bytes 1540
  171.3 44.6 %copy-start.11 = (f32[2,1,128]{2,1,0:T(1,128)S(1)}, f32[2,1,128]{2,1,0:T(1,128)}, u32[]{:S(2)}) copy-start(f32[2,1,128]{2,1,0:T(1,128)} %copy-done.10) | copy-start | bytes 3076
  171.3 44.6 %copy-start.15 = (f32[2,1,128]{2,1,0:T(1,128)S(1)}, f32[2,1,128]{2,1,0:T(1,128)}, u32[]{:S(2)}) copy-start(f32[2,1,128]{2,1,0:T(1,128)} %copy-done.14) | copy-start | bytes 3076
  171.3 45.4 %copy-start.7 = (f32[128,128]{1,0:T(8,128)S(1)}, f32[128,128]{1,0:T(8,128)}, u32[]{:S(2)}) copy-start(f32[128,128]{1,0:T(8,128)} %fusion.57) | copy-start | bytes 196612
  171.4 46.1 %copy-start.13 = (f32[2,1,128]{2,1,0:T(1,128)S(1)}, f32[2,1,128]{2,1,0:T(1,128)}, u32[]{:S(2)}) copy-start(f32[2,1,128]{2,1,0:T(1,128)} %copy-done.12) | copy-start | bytes 3076
  216.4 2.1 copy-start.20
  219.3 0.7 copy-start.19
  219.3 0.7 copy-start.23
  222.0 21.3 %copy-start.17 = (bf16[32,2]{0,1:T(2,128)(2,1)S(1)}, bf16[32,2]{0,1:T(2,128)(2,1)}, u32[]{:S(2)}) copy-start(bf16[32,2]{0,1:T(2,128)(2,1)} %copy-done.16) | copy-start | bytes 388
  222.0 21.3 %all-to-all-start.2 = ((bf16[32,1,128,128]{3,2,1,0:T(8,128)(2,1)}), bf16[32,1,128,128]{3,2,1,0:T(8,128)(2,1)S(1)}, u32[]{:S(2)}, u32[]{:S(2)}) async-start(bf16[32,1,128,128]{3,2,1,0:T(8,128)(2,1)} %copy.183), calls=%async_computation.2 | async-start | bytes 2097152 | tf_op jit(solution)/shard_map/all_to_all | solution.py:183
  226.1 274.9 %all-reduce.4.cloned.1.call-start = ((), (), s32[]{:S(2)}) async-start(), calls=%async_computation.3 | async-start | bytes 1048576 | tf_op jit(solution)/shard_map/psum | solution.py:112
  226.4 18.0 %copy-start.2 = (bf16[256,512]{1,0:T(8,128)(2,1)S(1)}, bf16[256,512]{1,0:T(8,128)(2,1)}, u32[]{:S(2)}) copy-start(bf16[256,512]{1,0:T(8,128)(2,1)} %copy-done.1) | copy-start | bytes 786436
  244.0 1.6 copy-start.4
  244.0 1.6 copy-start.27
  246.0 1.4 copy-start.8
  247.4 260.7 %copy-start.25 = (f32[512]{0:T(512)S(1)}, f32[512]{0:T(512)}, u32[]{:S(2)}) copy-start(f32[512]{0:T(512)} %param.10) | copy-start | bytes 6148
  501.0 7.6 %copy-start.6 = (f32[128,512]{0,1:T(8,128)S(1)}, f32[128,512]{0,1:T(8,128)}, u32[]{:S(2)}) copy-start(f32[128,512]{0,1:T(8,128)} %get-tuple-element.51) | copy-start | bytes 786436
  (1 other events, 0.6 us)
Sparse Core Ops, SparseCore 0:
  247.5 253.4 all-reduce.3
where the time goes:
time: 518 us; the launch traced here: 516 us
  waiting for transfers between devices  207 us (40%)
  other arithmetic  161 us (31%)
  blocking collectives  78.5 us (15%)
  starting transfers between devices  18.9 us (4%)
  matrix products  18.6 us (4%)
  between operations  16.8 us (3%)
  local copies, waits for them, and re-layouts  15.8 us (3%)
    psum x1, waiting for transfers between devices, apply_update(): lax.psum((gradients[0], gradients[1], gradients[2]), ('grp', 'blk'))  174 us
    psum x1, blocking collectives, apply_update(): lax.psum((gradients[0], gradients[1], gradients[2]), ('grp', 'blk'))  78.5 us
    another operation x8, other arithmetic, block_terms(): chol_c = jnp.linalg.cholesky(exp_cc + nugget * eye_c)  66.9 us
    another operation x10, other arithmetic, lower_solve(): lax.linalg.triangular_solve(factor_mat, right_side, left_side=True, lower...  60.9 us
    another operation x4, other arithmetic, block_terms(): chol_s = jnp.linalg.cholesky(schur_part)  24.3 us
    all_to_all x1, waiting for transfers between devices, shards(): lax.all_to_all(back_rows, 'blk', split_axis=0, concat_axis=0, tiled=True)  16.9 us
    all_to_all x1, waiting for transfers between devices, shards(): lax.all_to_all(send_rows, 'blk', split_axis=0, concat_axis=0, tiled=True)  14.6 us
  transfers between devices with their start and end apart: 4, of which 4 were waited for; matrix products, arithmetic and copies ran while one was open for 2% of the time, Pallas kernels for 0%

commit v1 on v0

v1 whole, which is shorter than its diff:
```python
import functools
import jax, jax.numpy as jnp
from jax import lax
from jax.experimental import pallas as pl
from jax.experimental.pallas import tpu as pltpu
f32=jnp.float32; bf16=jnp.bfloat16
PTS=128; HID=512; FEAT=128; ROWS=136

def split(x):
    hi=x.astype(bf16)
    return hi,(x-hi.astype(f32)).astype(bf16)

def mm(a,b):
    return lax.dot_general(a,b,(((1,),(0,)),((),())),preferred_element_type=f32)

def mm_t(a,b):
    return lax.dot_general(a,b,(((1,),(1,)),((),())),preferred_element_type=f32)

def t_mm(a,b):
    return lax.dot_general(a,b,(((0,),(0,)),((),())),preferred_element_type=f32)

def mm3(a,b):
    ah,al=split(a); bh,bl=split(b)
    return mm(jnp.concatenate([ah,al,ah],1),jnp.concatenate([bh,bh,bl],0))

def mm3_t(a,b):
    ah,al=split(a); bh,bl=split(b)
    return mm_t(jnp.concatenate([ah,al,ah],1),jnp.concatenate([bh,bh,bl],1))

def sweep(mats, GS=16):
    nb=len(mats); H=GS//8
    sub=lax.broadcasted_iota(jnp.int32,(8,128),0); lane8=lax.broadcasted_iota(jnp.int32,(8,128),1)
    lane=lax.broadcasted_iota(jnp.int32,(128,128),1)
    bc=lambda x,s: jnp.broadcast_to(x[s:s+1,:],(8,128))
    A=[m[0] for m in mats]; Y=[m[1] for m in mats]; W=[[] for _ in mats]
    for g in range(128//GS):
        c=GS*g
        pre=[]; a=[];y=[];w=[];cols=[]
        for b in range(nb):
            pre.append(split(A[b]))
            a.append([A[b][c+8*h:c+8*h+8,:] for h in range(H)])
            y.append([Y[b][c+8*h:c+8*h+8,:] for h in range(H)])
            w.append([y[b][h] for h in range(H)])
            cols.append([[jnp.broadcast_to(a[b][h][:,c+j:c+j+1],(8,128)) for h in range(H)] for j in range(GS)])
        for k in range(GS):
            h0,s=k//8,k%8
            for b in range(nb):
                d=bc(cols[b][k][h0],s); inv=1.0/d
                t=[cols[b][k][h]*inv for h in range(H)]
                t[h0]=jnp.where(sub==s,1.0-inv,t[h0])
                for h in range(H):
                    e=jnp.where(sub==s,1.0,0.0) if h==h0 else 0.0
                    a[b][h]=jnp.where(lane8==c+k,e,a[b][h])
                ra=bc(a[b][h0],s); ry=bc(y[b][h0],s)
                w[b][h0]=jnp.where(sub==s,ry*lax.rsqrt(d),w[b][h0])
                for j in range(k+1,GS):
                    rj=bc(cols[b][j][h0],s)
                    for h in range(H): cols[b][j][h]=cols[b][j][h]-t[h]*rj
                for h in range(H):
                    a[b][h]=a[b][h]-t[h]*ra
                    y[b][h]=y[b][h]-t[h]*ry
        for b in range(nb):
            Gr=jnp.concatenate([jnp.concatenate(a[b],0),jnp.concatenate(y[b],0)],1)
            gh,gl=split(Gr)
            z=lambda n: jnp.zeros((n,256),bf16)
            emb=lambda x: jnp.concatenate(([z(c)] if c else [])+[x]+([z(128-c-GS)] if 128-c-GS else []),0)
            eh=emb(gh); el=emb(gl); ah,al=pre[b]
            U=mm(jnp.concatenate([ah,al,ah],1),jnp.concatenate([eh,eh,el],0))
            inc=(lane>=c)&(lane<c+GS)
            An=jnp.where(inc,0.0,A[b])-U[:,:128]; Yn=Y[b]-U[:,128:]
            put=lambda full,part: jnp.concatenate(([full[:c]] if c else [])+[part]+([full[c+GS:]] if c+GS<128 else []),0)
            A[b]=put(An,Gr[:,:128]); Y[b]=put(Yn,Gr[:,128:])
            W[b]+=w[b]
    return [(A[b],Y[b],jnp.concatenate(W[b],0)) for b in range(nb)]

def local_kernel(weight, allx_ref, win_ref, bin_ref, wout_ref, w_out, pk_out,
                 x_s, hid_s, slope_s, f_s, e_s, a_s, y_s, cot_s):
    NB=2
    win16=win_ref[...].astype(bf16); wout16=wout_ref[...].astype(bf16); bias=bin_ref[...]
    eye=(lax.broadcasted_iota(jnp.int32,(128,128),0)==lax.broadcasted_iota(jnp.int32,(128,128),1))
    ones=jnp.ones((128,128),bf16)
    for i in range(6):
        b,j=divmod(i,3)
        blk=allx_ref[i]
        x=blk[:128,:]
        x_s[pl.ds(128*i,128),:]=x
        yrow=blk[128:136,:].astype(f32)[0:1,:]
        diag=jnp.where(eye,jnp.broadcast_to(yrow,(128,128)),0.0).astype(bf16)
        y_s[b,j]=mm(diag,ones)
        pre=mm(x,win16)+bias
        s=1.0/(1.0+jnp.exp(-pre))
        hid=(pre*s).astype(bf16)
        slope_s[pl.ds(128*i,128),:]=s*(1.0+pre*(1.0-s))
        hid_s[pl.ds(128*i,128),:]=hid
        f_s[pl.ds(128*i,128),:]=mm(hid,wout16).astype(bf16)
    for b in range(NB):
        F=f_s[pl.ds(384*b,384),:]; Ff=F.astype(f32)
        FF=Ff*Ff
        sqc=jnp.sum(FF,axis=1,keepdims=True)
        fh,fl=split(FF)
        o8=jnp.ones((8,128),bf16)
        sqr=(mm_t(o8,fh)+mm_t(o8,fl))[0:1,:]
        cross=mm_t(F,F)
        E=jnp.exp((sqc+sqr-2.0*cross)*(-2.0/FEAT))
        for i in range(3):
            for j in range(3):
                t=E[128*i:128*i+128,128*j:128*j+128]
                e_s[b,i,j]=t
                a_s[b,i,j]=jnp.where(eye,t+0.5,t) if i==j else t
    r=sweep([(a_s[b,0,0],y_s[b,0]) for b in range(NB)])
    for b in range(NB):
        D,Y1,_=r[b]
        Hm=mm3(D,jnp.concatenate([a_s[b,0,1],a_s[b,0,2]],1))
        R=jnp.concatenate([Hm,Y1],1)
        L=jnp.concatenate([a_s[b,1,0],a_s[b,2,0]],0)
        U=mm3(L,R)
        a_s[b,1,1]=a_s[b,1,1]-U[:128,:128]
        a_s[b,1,2]=a_s[b,1,2]-U[:128,128:256]
        a_s[b,2,1]=a_s[b,2,1]-U[128:,:128]
        a_s[b,2,2]=a_s[b,2,2]-U[128:,128:256]
        y_s[b,1]=y_s[b,1]-U[:128,256:]
        y_s[b,2]=y_s[b,2]-U[128:,256:]
        a_s[b,0,1]=Hm[:,:128]; a_s[b,0,2]=Hm[:,128:]; y_s[b,0]=Y1
    r=sweep([(a_s[b,1,1],y_s[b,1]) for b in range(NB)])
    for b in range(NB):
        D,Y2,_=r[b]
        Hb=mm3(D,a_s[b,1,2])
        L=jnp.concatenate([a_s[b,0,1],a_s[b,2,1]],0)
        U=mm3(L,jnp.concatenate([Hb,Y2],1))
        a_s[b,0,2]=a_s[b,0,2]-U[:128,:128]
        a_s[b,1,2]=Hb
        a_s[b,2,2]=a_s[b,2,2]-U[128:,:128]
        y_s[b,0]=y_s[b,0]-U[:128,128:]
        y_s[b,1]=Y2
        y_s[b,2]=y_s[b,2]-U[128:,128:]
    r=sweep([(a_s[b,2,2],y_s[b,2]) for b in range(NB)])
    torow=lambda Y: jnp.sum(jnp.where(eye,Y,0.0),axis=0,keepdims=True)
    for b in range(NB):
        D,ab,W=r[b]
        w_out[pl.ds(b,1),:]=torow(W)
        G=jnp.concatenate([a_s[b,0,2],a_s[b,1,2]],0)
        v=jnp.concatenate([y_s[b,0],y_s[b,1]],0)
        Pa=mm3(G,jnp.concatenate([D,ab],1))
        Pm=Pa[:,:128]; ac=v-Pa[:,128:]
        PT=mm3_t(D,G)
        Z=mm3_t(Pm,G)
        abr=torow(ab); acr=[torow(ac[:128]),torow(ac[128:])]; vr=[torow(v[:128]),torow(v[128:])]
        acs=[ac[:128],ac[128:]]; vs=[v[:128],v[128:]]
        rows=[]
        for i in range(3):
            row=[]
            for j in range(3):
                if i<2 and j<2: gm=Z[128*i:128*i+128,128*j:128*j+128]-acs[i]*acr[j]+vs[i]*vr[j]
                elif i<2: gm=-Pm[128*i:128*i+128,:]-acs[i]*abr
                elif j<2: gm=-PT[:,128*j:128*j+128]-ab*acr[j]
                else: gm=D-ab*abr
                t=0.5*gm*e_s[b,i,j]
                if i==j: t=jnp.where(eye,0.0,t)
                row.append(t)
            rows.append(jnp.concatenate(row,1))
        em=jnp.concatenate(rows,0)
        eh,el=split(em)
        F=f_s[pl.ds(384*b,384),:]
        Fo=jnp.concatenate([F,jnp.ones((384,128),bf16)],1)
        ef=mm(jnp.concatenate([eh,el],1),jnp.concatenate([Fo,Fo],0))
        cot_s[pl.ds(384*b,384),:]=((-8.0*weight/FEAT)*(ef[:,128:]*F.astype(f32)-ef[:,:128])).astype(bf16)
    cot=cot_s[...]
    backed=mm_t(cot,wout16)*slope_s[...]
    gin=t_mm(x_s[...],backed.astype(bf16)).astype(bf16)
    gout=t_mm(cot,hid_s[...]).astype(bf16)
    gb=jnp.sum(backed,axis=0,keepdims=True).astype(bf16)
    gb8=jnp.concatenate([gb[:,128*i:128*i+128] for i in range(4)]+[jnp.zeros((4,128),bf16)],0)
    for i in range(16):
        pk_out[i]=jnp.concatenate([gin[8*i:8*i+8,:],gb8],1)
        pk_out[16+i]=jnp.concatenate([gout[8*i:8*i+8,:],gb8],1)

def local_call(blocks, win, bin_, wout, weight):
    V=pltpu.VMEM
    return pl.pallas_call(
        functools.partial(local_kernel, weight),
        out_shape=(jax.ShapeDtypeStruct((2,128),f32),jax.ShapeDtypeStruct((32,8,640),bf16)),
        in_specs=[pl.BlockSpec(memory_space=V)]*4,
        out_specs=(pl.BlockSpec(memory_space=V),)*2,
        scratch_shapes=[V((768,128),bf16),V((768,512),bf16),V((768,512),f32),V((768,128),bf16),V((2,3,3,128,128),f32),V((2,3,3,128,128),f32),V((2,3,128,128),f32),V((768,128),bf16)],
        name="local_terms",
    )(blocks,win,bin_,wout)


from jax.sharding import PartitionSpec as P

MESH = pl.DeviceIdType.MESH
CHUNKS = 32


def remote(src, dst, send_sem, recv_sem, device):
    return pltpu.make_async_remote_copy(
        src_ref=src, dst_ref=dst, send_sem=send_sem, recv_sem=recv_sem,
        device_id=device, device_id_type=MESH,
    )


def gather_kernel(idx_ref, own_ref, out_ref, buf, send_sem, recv_sem, local_sem):
    me = lax.axis_index("blk")
    here = (me // 8, (me // 2) % 4)
    core = me % 2
    partner = me + 1 - 2 * core
    sign = 1 - 2 * core

    def peer(first, dp, dq):
        p = (here[first] + dp + 4) % 4
        q = (here[1 - first] + dq + 4) % 4
        yy, xx = (p, q) if first == 0 else (q, p)
        return yy * 8 + xx * 2 + core

    barrier = pltpu.get_barrier_semaphore()
    near = [peer(0, 1, 0), peer(0, 3, 0), peer(0, 0, 1), peer(0, 0, 3), partner]
    for dev in near:
        pl.semaphore_signal(barrier, inc=1, device_id={"blk": dev}, device_id_type=MESH)
    pl.semaphore_wait(barrier, len(near))

    sends = []

    def push(src, slot, half, dev, sem):
        cp = remote(src, buf.at[slot, half], send_sem.at[half, sem], recv_sem.at[half, sem], {"blk": dev})
        cp.start()
        sends.append(cp)

    def arrive(slot, half, sem):
        remote(
            buf.at[slot, half], buf.at[slot, half], send_sem.at[half, sem], recv_sem.at[half, sem],
            {"blk": partner},
        ).wait_recv()

    locals_ = []
    for h in range(2):
        cp = pltpu.make_async_copy(own_ref.at[h], buf.at[me, h], local_sem.at[h])
        cp.start()
        locals_.append(cp)

    offs = (0, 1, 3, 2)
    turn = (1, -1, -1, 1)

    def spread(src, slot, half, i):
        first = 1 - half
        push(src, slot, half, peer(first, 0, 1), 3 + 2 * i)
        push(src, slot, half, peer(first, 0, 3), 4 + 2 * i)

    def relay(src, slot, half, i, j):
        push(src, slot, half, partner, 15 + 4 * i + j)

    for h in range(2):
        first = 1 - h
        push(own_ref.at[h], me, h, peer(first, 1, 0), 0)
        push(own_ref.at[h], me, h, peer(first, 3, 0), 1)
    for h in range(2):
        spread(own_ref.at[h], me, h, 0)
        relay(own_ref.at[h], me, h, 0, 0)
    for h in range(2):
        first = 1 - h
        behind, ahead = peer(first, 3, 0), peer(first, 1, 0)
        arrive(behind, h, 0)
        arrive(ahead, h, 1)
        passed = peer(first, 4 - sign, 0)
        push(buf.at[passed, h], passed, h, peer(first, 4 + sign, 0), 2)
        for i, slot in ((1, ahead), (2, behind)):
            spread(buf.at[slot, h], slot, h, i)
            relay(buf.at[slot, h], slot, h, i, 0)

    def second(h, i):
        first = 1 - h
        s_ = turn[i]
        behind, ahead = peer(first, offs[i], 3), peer(first, offs[i], 1)
        arrive(behind, h, 3 + 2 * i)
        arrive(ahead, h, 4 + 2 * i)
        passed = behind if s_ == 1 else ahead
        push(buf.at[passed, h], passed, h, peer(first, 0, s_ % 4), 11 + i)
        relay(buf.at[ahead, h], ahead, h, i, 1)
        relay(buf.at[behind, h], behind, h, i, 3)

    for h in range(2):
        second(h, 0)
    for h in range(2):
        first = 1 - h
        far = peer(first, 2, 0)
        arrive(far, h, 2)
        spread(buf.at[far, h], far, h, 3)
        relay(buf.at[far, h], far, h, 3, 0)
    for i in (1, 2, 3):
        for h in range(2):
            second(h, i)
    for i in range(4):
        for h in range(2):
            far = peer(1 - h, offs[i], 2)
            arrive(far, h, 11 + i)
            relay(buf.at[far, h], far, h, i, 2)
    for i in range(4):
        for h in range(2):
            for j in range(4):
                slot = peer(1 - h, offs[i], (0, 1, 2, 3)[j]) + 1 - 2 * core
                arrive(slot, h, 15 + 4 * i + j)
    for cp in locals_:
        cp.wait()
    for n in range(2):
        out_ref[3 * n + 2] = own_ref[n]
        for j in range(2):
            at = idx_ref[2 * n + j]
            out_ref[3 * n + j] = buf[at // 2, at % 2]
    for cp in sends:
        cp.wait_send()


def gather_call(idx, own):
    V = pltpu.VMEM
    return pl.pallas_call(
        gather_kernel,
        out_shape=jax.ShapeDtypeStruct((6, ROWS, 128), bf16),
        in_specs=[pl.BlockSpec(memory_space=pltpu.SMEM), pl.BlockSpec(memory_space=V)],
        out_specs=pl.BlockSpec(memory_space=V),
        scratch_shapes=[
            V((32, 2, ROWS, 128), bf16),
            pltpu.SemaphoreType.DMA((2, 31)),
            pltpu.SemaphoreType.DMA((2, 31)),
            pltpu.SemaphoreType.DMA((2,)),
        ],
        compiler_params=pltpu.CompilerParams(collective_id=0, has_side_effects=True),
        name="gather_blocks",
    )(idx, own)


def reduce_kernel(pk_ref, win_ref, bin_ref, wout_ref, in_out, bias_out, out_out,
                  rs_buf, part, z_buf, ag_buf, final, rs_send, rs_recv, z_send, z_recv, ag_send, ag_recv):
    me = lax.axis_index("blk")
    z = lax.axis_index("grp")
    barrier = pltpu.get_barrier_semaphore()
    plane = [(me + o) % 32 for o in range(1, 32)]
    column = [(z + o) % 8 for o in range(1, 8)]
    for dev in plane:
        pl.semaphore_signal(barrier, inc=1, device_id={"blk": dev}, device_id_type=MESH)
    for dev in column:
        pl.semaphore_signal(barrier, inc=1, device_id={"grp": dev}, device_id_type=MESH)
    pl.semaphore_wait(barrier, 38)
    sends = []

    def push(src, dst, ss, rs, dev):
        cp = remote(src, dst, ss, rs, dev)
        cp.start()
        sends.append(cp)

    for o, dev in enumerate(plane):
        push(pk_ref.at[dev], rs_buf.at[me], rs_send.at[o], rs_recv.at[o], {"blk": dev})
    rs_buf[me] = pk_ref[me]
    for o in range(31):
        src = (me + 31 - o) % 32
        remote(pk_ref.at[src], rs_buf.at[src], rs_send.at[o], rs_recv.at[o], {"blk": src}).wait_recv()
    acc = rs_buf[0].astype(f32)
    for i in range(1, 32):
        acc = acc + rs_buf[i].astype(f32)
    part[...] = acc.astype(bf16)
    z_buf[z] = acc.astype(bf16)
    for o, dev in enumerate(column):
        push(part, z_buf.at[z], z_send.at[o], z_recv.at[o], {"grp": dev})
    for o in range(7):
        src = (z + 7 - o) % 8
        remote(part, z_buf.at[src], z_send.at[o], z_recv.at[o], {"grp": src}).wait_recv()
    acc = z_buf[0].astype(f32)
    for i in range(1, 8):
        acc = acc + z_buf[i].astype(f32)
    done = acc[:, :512].astype(bf16)
    bias = acc[:4, 512:]
    final[...] = done
    ag_buf[me] = done
    for o, dev in enumerate(plane):
        push(final, ag_buf.at[me], ag_send.at[o], ag_recv.at[o], {"blk": dev})
    for o in range(31):
        src = (me + 31 - o) % 32
        remote(final, ag_buf.at[src], ag_send.at[o], ag_recv.at[o], {"blk": src}).wait_recv()
    total = jnp.zeros((8, 512), f32)
    for i in range(32):
        t = ag_buf[i].astype(f32)
        total = total + t * t
    squares = jnp.sum(total) + jnp.sum(bias * bias)
    scale = 3.0 / jnp.sqrt(jnp.broadcast_to(squares, (1, 1)) + 1e-06)
    bias_out[...] = bin_ref[...] - scale * bias
    for i in range(16):
        in_out[pl.ds(8 * i, 8), :] = win_ref[pl.ds(8 * i, 8), :] - scale * ag_buf[i].astype(f32)
    for q in range(4):
        t = jnp.concatenate([ag_buf[16 + i][:, 128 * q:128 * q + 128].astype(f32) for i in range(16)], 0)
        out_out[pl.ds(128 * q, 128), :] = wout_ref[pl.ds(128 * q, 128), :] - scale * jnp.transpose(t)
    for cp in sends:
        cp.wait_send()


def reduce_call(pk, win, bias, wout):
    V = pltpu.VMEM
    D = pltpu.SemaphoreType.DMA
    return pl.pallas_call(
        reduce_kernel,
        out_shape=(
            jax.ShapeDtypeStruct((128, 512), f32),
            jax.ShapeDtypeStruct((4, 128), f32),
            jax.ShapeDtypeStruct((512, 128), f32),
        ),
        in_specs=[pl.BlockSpec(memory_space=V)] * 4,
        out_specs=(pl.BlockSpec(memory_space=V),) * 3,
        scratch_shapes=[
            V((32, 8, 640), bf16), V((8, 640), bf16), V((8, 8, 640), bf16),
            V((32, 8, 512), bf16), V((8, 512), bf16),
            D((31,)), D((31,)), D((7,)), D((7,)), D((31,)), D((31,)),
        ],
        compiler_params=pltpu.CompilerParams(collective_id=1, has_side_effects=True),
        name="sum_gradients",
    )(pk, win, bias, wout)


def shards(inputs, targets, weight_in, bias_in, weight_out, neighbors, owner_map):
    me = lax.axis_index("blk")
    region = lax.axis_index("grp")
    first = region * 64
    ids = lax.dynamic_slice_in_dim(neighbors, first + 2 * me, 2, 0).reshape(-1)
    idx = jnp.take(owner_map, ids, axis=0) - first
    own = jnp.concatenate(
        [inputs.reshape(2, PTS, 128), jnp.pad(targets.reshape(2, 1, PTS), ((0, 0), (0, 7), (0, 0)))], 1
    )
    blocks = gather_call(idx, own)
    white, packed = local_call(blocks, weight_in, bias_in.reshape(1, -1), weight_out, 1.0 / neighbors.shape[0])
    new_in, new_bias, new_out = reduce_call(packed, weight_in, bias_in.reshape(4, 128), weight_out)
    return (white.reshape(-1), new_in, new_bias.reshape(-1), new_out)


def solution(mesh):
    placed = (P(("grp", "blk"), None), P(("grp", "blk")), P(), P(), P(), P(), P())
    return jax.shard_map(
        shards,
        mesh=mesh,
        in_specs=placed,
        out_specs=(P(("grp", "blk")), P(), P(), P()),
        check_vma=False,
    )
```

time: 518 us -> 78.9 us (0.15)
  waiting for transfers between devices: 207 us -> 0 us
  other arithmetic: 161 us -> 1.16 us
  blocking collectives: 78.5 us -> 0 us
  Pallas kernels: 0 us -> 70.8 us
  starting transfers between devices: 18.9 us -> 0 us
  matrix products: 18.6 us -> 0 us
  between operations: 16.8 us -> 0.69 us
  local copies, waits for them, and re-layouts: 15.8 us -> 5.99 us
    psum x1 -> x0, waiting for transfers between devices: 174 us -> none  [apply_update(): lax.psum((gradients[0], gradients[1], gradients[2]), ('grp', 'blk'))]
    another operation x22 -> x0, other arithmetic: 152 us -> none  [the longest x8 66.9 us: block_terms(): chol_c = jnp.linalg.cholesky(exp_cc + nugget * eye_c)]
    psum x1 -> x0, blocking collectives: 78.5 us -> none  [apply_update(): lax.psum((gradients[0], gradients[1], gradients[2]), ('grp', 'blk'))]
    pallas_call x0 -> x3, Pallas kernels: none -> 70.8 us  [the longest x1 27.2 us: reduce_call(): pl.pallas_call(reduce_kernel, out_shape=(jax.ShapeDtypeStruct((128, 512),...]
    all_to_all x3 -> x0, waiting for transfers between devices: 32.7 us -> none  [the longest x1 16.9 us: shards(): lax.all_to_all(back_rows, 'blk', split_axis=0, concat_axis=0, tiled=True)]
    all_to_all x3 -> x0, starting transfers between devices: 18.8 us -> none  [the longest x1 8.58 us: shards(): lax.all_to_all(send_targets, 'blk', split_axis=0, concat_axis=0, tiled=True)]
    dot_general x22 -> x0, matrix products: 13.5 us -> none  [the longest x1 2.03 us: features_of(): jnp.dot(rows_in, weight_in16, preferred_element_type=jnp.float32) + bias_now]
    another operation x11 -> x0, local copies, waits for them, and re-layouts: 5.5 us -> none
  transfers between devices with their start and end apart: 4 -> 0, of which waited for: 4 -> 0; matrix products, arithmetic and copies ran while one was open for 2% -> 0% of each run, Pallas kernels for 0% -> 0%
where the time goes in v1:
time: 78.9 us; the launch traced here: 78.7 us
  Pallas kernels  70.8 us (90%)
  local copies, waits for them, and re-layouts  5.99 us (8%)
  other arithmetic  1.16 us (1%)
    pallas_call x1, Pallas kernels, reduce_call(): pl.pallas_call(reduce_kernel, out_shape=(jax.ShapeDtypeStruct((128, 512),...  27.2 us
    pallas_call x1, Pallas kernels, gather_call(): pl.pallas_call(gather_kernel, out_shape=jax.ShapeDtypeStruct((6, ROWS, 12...  23.7 us
    pallas_call x1, Pallas kernels, local_call(): pl.pallas_call(functools.partial(local_kernel, weight), out_shape=(jax.Sh...  19.9 us
    unnamed x15, local copies, waits for them, and re-layouts  5.01 us

profile of v1, /device:TPU:1, one launch (start us, length us, event | category | flops | bytes accessed | tf_op | source)
XLA Modules:
  0.0 78.7 jit_solution(2439924109032216117)
XLA Ops:
  0.6 0.0 copy-start
  0.7 0.7 copy-done
  1.3 0.1 constant_dynamic-slice_fusion
  1.4 0.1 copy.13
  1.5 0.1 reshape.66
  1.6 0.1 reshape.65
  1.7 0.0 copy-start.5
  1.7 0.6 copy-done.5
  2.3 0.0 copy-start.1
  2.3 0.7 copy-done.1
  3.0 0.0 copy-start.3
  3.0 0.6 gather_fusion
  3.6 0.5 fusion.3.idx_ref
  4.2 0.0 copy-done.3
  4.2 0.6 fusion.1.own_ref
  4.8 23.7 %gather_blocks.1.allx_ref = bf16[6,136,128]{2,1,0:T(8,128)(2,1)} custom-call(s32[4]{0:T(128)} %fusion.3.idx_ref, bf16[2,136,128]{2,1,0:T(8,128)(2,1)} %fusion.1.own_ref), custom_call_target="tpu_custom_call" | custom-call | tf_op jit(solution)/shard_map/gather_blocks/pallas_call | solution.py:314
  28.5 19.9 %local_terms.1 = (f32[2,128]{1,0:T(2,128)}, bf16[32,8,640]{2,1,0:T(8,128)(2,1)}) custom-call(bf16[6,136,128]{2,1,0:T(8,128)(2,1)} %gather_blocks.1.allx_ref, f32[128,512]{1,0:T(8,128)} %win_ref.3, f32[1,512]{1,0:T(1,128)} %bitcast.9, f32[512,128]{1,0:T(8,128)} %wout_ref.3), custom_call_target="tpu_custom_call" | custom-call | tf_op jit(solution)/shard_map/local_terms/pallas_call | solution.py:179
  48.5 27.2 %sum_gradients.1 = (f32[128,512]{1,0:T(8,128)}, f32[4,128]{1,0:T(4,128)}, f32[512,128]{1,0:T(8,128)}) custom-call(bf16[32,8,640]{2,1,0:T(8,128)(2,1)} %get-tuple-element.10.pk_ref, f32[128,512]{1,0:T(8,128)} %win_ref.3, f32[4,128]{1,0:T(4,128)} %bitcast.10, f32[512,128]{1,0:T(8,128)} %wout_ref.3), custom_call_target="tpu_custom_call" | custom-call | tf_op jit(solution)/shard_map/sum_gradients/pallas_call | solution.py:396
  75.6 0.0 copy-start.4
  75.6 0.0 copy-start.2
  75.6 1.7 %copy.19 = f32[128,512]{1,0:T(8,128)} copy(f32[128,512]{1,0:T(8,128)} %get-tuple-element.19) | data formatting | bytes 524288
  77.4 0.0 copy-done.4
  77.4 0.6 copy.20
  77.9 0.0 copy-done.2
  77.9 0.7 copy.21
  (3 shorter events, 0.0 us)
Async XLA Ops:
  0.6 0.7 copy-start
  1.7 0.7 copy-start.5
  2.3 0.7 copy-start.1
  3.0 1.2 %copy-start.3 = (bf16[256,128]{1,0:T(8,128)(2,1)S(1)}, bf16[256,128]{1,0:T(8,128)(2,1)}, u32[]{:S(2)}) copy-start(bf16[256,128]{1,0:T(8,128)(2,1)} %param.7) | copy-start | bytes 196612
  75.6 1.7 %copy-start.4 = (f32[4,128]{1,0:T(4,128)S(1)}, f32[4,128]{1,0:T(4,128)}, u32[]{:S(2)}) copy-start(f32[4,128]{1,0:T(4,128)} %get-tuple-element.12) | copy-start | bytes 6148
  75.6 2.3 %copy-start.2 = (f32[512,128]{1,0:T(8,128)S(1)}, f32[512,128]{1,0:T(8,128)}, u32[]{:S(2)}) copy-start(f32[512,128]{1,0:T(8,128)} %get-tuple-element.21) | copy-start | bytes 786436

commit v2 on v0

v2 whole, which is shorter than its diff:
```python
import functools
import jax, jax.numpy as jnp
from jax import lax
from jax.experimental import pallas as pl
from jax.experimental.pallas import tpu as pltpu
from jax.sharding import PartitionSpec as P
f32=jnp.float32; bf16=jnp.bfloat16
PTS=128; HID=512; FEAT=128; ROWS=136

def split(x):
    hi=x.astype(bf16)
    return hi,(x-hi.astype(f32)).astype(bf16)

def mm(a,b):
    return lax.dot_general(a,b,(((1,),(0,)),((),())),preferred_element_type=f32)

def mm_t(a,b):
    return lax.dot_general(a,b,(((1,),(1,)),((),())),preferred_element_type=f32)

def t_mm(a,b):
    return lax.dot_general(a,b,(((0,),(0,)),((),())),preferred_element_type=f32)

def mm3(a,b):
    ah,al=split(a); bh,bl=split(b)
    return mm(jnp.concatenate([ah,al,ah],1),jnp.concatenate([bh,bh,bl],0))

def mm3_t(a,b):
    ah,al=split(a); bh,bl=split(b)
    return mm_t(jnp.concatenate([ah,al,ah],1),jnp.concatenate([bh,bh,bl],1))

LOW, HIGH, DOUBLINGS = 0.5, 128.5, 6


def inverses(mats):
    eye = lax.broadcasted_iota(jnp.int32, (128, 128), 0) == lax.broadcasted_iota(jnp.int32, (128, 128), 1)
    ident = jnp.where(eye, 1.0, 0.0)
    centre = (HIGH + LOW) / (HIGH - LOW)
    first = 2.0 / (HIGH + LOW)
    res = [ident - first * m for m in mats]
    inv = [first * ident for m in mats]
    tau = centre
    for step in range(DOUBLINGS):
        twice = 2.0 * tau * tau - 1.0
        gain = 2.0 * tau * tau / twice
        shift = 1.0 / twice
        if step == 0:
            prods = [mm3(r, r) for r in res]
            inv = [(gain * first) * (ident + r) for r in res]
            res = [gain * p - shift * ident for p in prods]
        elif step < DOUBLINGS - 1:
            prods = [mm3(jnp.concatenate([r, x], 0), r) for r, x in zip(res, inv)]
            inv = [gain * (x + p[128:]) for x, p in zip(inv, prods)]
            res = [gain * p[:128] - shift * ident for p in prods]
        else:
            inv = [gain * (x + mm3(x, r)) for x, r in zip(inv, res)]
        tau = twice
    left = [ident - mm3(m, x) for m, x in zip(mats, inv)]
    return [x + mm3(x, r) for x, r in zip(inv, left)]


MESH = pl.DeviceIdType.MESH
V = pltpu.VMEM


def eliminate_group(mats, rows):
    nb = len(mats)
    sub = lax.broadcasted_iota(jnp.int32, (8, 128), 0)
    spread = lambda x, s: jnp.broadcast_to(x[s:s + 1, :], (8, 128))
    a = [[m[8 * h:8 * h + 8, :] for h in range(2)] for m in mats]
    y = [[r[8 * h:8 * h + 8, :] for h in range(2)] for r in rows]
    w = [[r[8 * h:8 * h + 8, :] for h in range(2)] for r in rows]
    cols = [[[jnp.broadcast_to(a[b][h][:, j:j + 1], (8, 128)) for h in range(2)] for j in range(16)] for b in range(nb)]
    for k in range(16):
        h0, s = divmod(k, 8)
        for b in range(nb):
            d = spread(cols[b][k][h0], s)
            inv = 1.0 / d
            t = [cols[b][k][h] * inv for h in range(2)]
            t[h0] = jnp.where(sub == s, 1.0 - inv, t[h0])
            ra = spread(a[b][h0], s)
            ry = spread(y[b][h0], s)
            w[b][h0] = jnp.where(sub == s, ry * lax.rsqrt(d), w[b][h0])
            for j in range(k + 1, 16):
                rj = spread(cols[b][j][h0], s)
                for h in range(2):
                    cols[b][j][h] = cols[b][j][h] - t[h] * rj
            for h in range(2):
                a[b][h] = a[b][h] - t[h] * ra
                y[b][h] = y[b][h] - t[h] * ry
    out = []
    for b in range(nb):
        done = jnp.concatenate([jnp.concatenate(a[b], 0), jnp.concatenate(y[b], 0)], 1)
        dh, dl = split(done)
        pad = jnp.zeros((112, 256), bf16)
        dh = jnp.concatenate([dh, pad], 0)
        dl = jnp.concatenate([dl, pad], 0)
        ah, al = split(mats[b])
        upd = mm(jnp.concatenate([ah, al, ah], 1), jnp.concatenate([dh, dh, dl], 0))
        rest = jnp.concatenate([mats[b][16:] - upd[16:, :128], done[:, :128]], 0)
        side = jnp.concatenate([rows[b][16:] - upd[16:, 128:], done[:, 128:]], 0)
        out.append((pltpu.roll(rest, 112, 1), side, jnp.concatenate(w[b], 0)))
    return out


def main_kernel(weight, nb_ref, om_ref, x_ref, t_ref, win_ref, bin_ref, wout_ref,
                w_out, tot_out, bias_out,
                buf, give, take, x_s, hid_s, slope_s, f_s, e_s, a_s, y_s, cot_s, sw_s, sr_s, ww_s,
                pk, rs_buf, part, z_buf, ag_buf,
                g_send, g_recv, d_sem, rs_send, rs_recv, z_send, z_recv, ag_send, ag_recv):
    me = lax.axis_index("blk")
    z = lax.axis_index("grp")
    here = (me // 8, (me // 2) % 4)
    core = me % 2
    partner = me + 1 - 2 * core
    chip = me // 2

    def chip_at(first, dp, dq):
        p = (here[first] + dp) % 4
        q = (here[1 - first] + dq) % 4
        return p * 4 + q if first == 0 else q * 4 + p

    def peer(first, dp, dq):
        return 2 * chip_at(first, dp, dq) + core

    sends = []

    def push(src, dst, ss, rs, dev):
        cp = pltpu.make_async_remote_copy(
            src_ref=src, dst_ref=dst, send_sem=ss, recv_sem=rs, device_id=dev, device_id_type=MESH
        )
        cp.start()
        sends.append(cp)

    def arrive(dst, ss, rs, dev):
        pltpu.make_async_remote_copy(
            src_ref=dst, dst_ref=dst, send_sem=ss, recv_sem=rs, device_id=dev, device_id_type=MESH
        ).wait_recv()

    barrier = pltpu.get_barrier_semaphore()
    near = [{"blk": peer(f, d, 0)} for f in range(2) for d in (1, 2, 3)] + [{"blk": partner}]
    column = [(z + o) % 8 for o in range(1, 8)]
    greeted = near + [{"grp": d} for d in column]
    for dev in greeted:
        pl.semaphore_signal(barrier, inc=1, device_id=dev, device_id_type=MESH)

    for h in range(2):
        buf[chip, h, pl.ds(0, 128), :] = x_ref[pl.ds(128 * h, 128), :]
        buf[chip, h, pl.ds(128, 8), :] = jnp.broadcast_to(t_ref[pl.ds(h, 1), :].astype(f32), (8, 128)).astype(bf16)
    pl.semaphore_wait(barrier, len(greeted))

    def fan(h, at, axis, base):
        for n, d in ((2, 2), (0, 1), (1, 3)):
            dev = peer(axis, d, 0)
            push(buf.at[at, h], buf.at[at, h], g_send.at[h, base + n], g_recv.at[h, base + n], {"blk": dev})

    def got(h, at, sem):
        arrive(buf.at[at, h], g_send.at[h, sem], g_recv.at[h, sem], {"blk": partner})

    firsts = (1, 0)
    for h in range(2):
        fan(h, chip, firsts[h], 0)
    for h in range(2):
        fan(h, chip, 1 - firsts[h], 3)

    win16 = win_ref[...].astype(bf16)
    wout16 = wout_ref[...].astype(bf16)
    bias = bin_ref[...]
    eye = lax.broadcasted_iota(jnp.int32, (128, 128), 0) == lax.broadcasted_iota(jnp.int32, (128, 128), 1)
    ones = jnp.ones((128, 128), bf16)

    def forward(i, blk):
        x = blk[:128, :]
        x_s[pl.ds(128 * i, 128), :] = x
        yrow = blk[128:136, :].astype(f32)[0:1, :]
        diag = jnp.where(eye, jnp.broadcast_to(yrow, (128, 128)), 0.0).astype(bf16)
        y_s[i] = mm(diag, ones)
        pre = mm(x, win16) + bias
        s = 1.0 / (1.0 + jnp.exp(-pre))
        hid = (pre * s).astype(bf16)
        slope_s[pl.ds(128 * i, 128), :] = s * (1.0 + pre * (1.0 - s))
        hid_s[pl.ds(128 * i, 128), :] = hid
        f_s[pl.ds(128 * i, 128), :] = mm(hid, wout16).astype(bf16)

    origin = {0: 3, 1: 1, 2: 2}
    for n in (0, 1, 2):
        for h in range(2):
            at = chip_at(firsts[h], origin[n], 0)
            got(h, at, n)
            fan(h, at, 1 - firsts[h], 6 + 3 * n)
    for h in range(2):
        forward(3 * h + 2, buf[chip, h])
    for k in range(4):
        for n in (0, 1, 2):
            for h in range(2):
                dp = 0 if k == 0 else origin[k - 1]
                got(h, chip_at(firsts[h], dp, origin[n]), 3 + 3 * k + n)

    base = 64 * z

    def wanted(dev, n, j):
        pos = om_ref[nb_ref[j, base + 2 * dev + n]] % 64
        return pos // 4, (pos // 2) % 2, pos % 2

    for n in range(2):
        for j in range(2):
            at, unused, half = wanted(partner, n, j)
            give[2 * n + j] = buf[at, half]
    push(give, take, d_sem.at[0], d_sem.at[1], {"blk": partner})
    mine = []
    for n in range(2):
        for j in range(2):
            at, owner, half = wanted(me, n, j)
            mine.append((buf[at, half], owner))
    arrive(take, d_sem.at[0], d_sem.at[1], {"blk": partner})
    for n in range(2):
        for j in range(2):
            blk, owner = mine[2 * n + j]
            same = jnp.broadcast_to(owner, (ROWS, 128)) == core
            forward(3 * n + j, jnp.where(same, blk.astype(f32), take[2 * n + j].astype(f32)).astype(bf16))

    NB = 2
    for b in range(NB):
        F = f_s[pl.ds(384 * b, 384), :]
        Ff = F.astype(f32)
        FF = Ff * Ff
        sqc = jnp.sum(FF, axis=1, keepdims=True)
        fh, fl = split(FF)
        o8 = jnp.ones((8, 128), bf16)
        sqr = (mm_t(o8, fh) + mm_t(o8, fl))[0:1, :]
        cross = mm_t(F, F)
        E = jnp.exp((sqc + sqr - 2.0 * cross) * (-2.0 / FEAT))
        for i in range(3):
            for j in range(3):
                t = E[128 * i:128 * i + 128, 128 * j:128 * j + 128]
                e_s[b, i, j] = t
                a_s[b, i, j] = jnp.where(eye, t + 0.5, t) if i == j else t
    Y = lambda b, i: 3 * b + i
    r = inverses([a_s[b, 0, 0] for b in range(NB)])
    for b in range(NB):
        R = mm3(r[b], jnp.concatenate([a_s[b, 0, 1], a_s[b, 0, 2], y_s[Y(b, 0)]], 1))
        U = mm3(jnp.concatenate([a_s[b, 1, 0], a_s[b, 2, 0]], 0), R)
        a_s[b, 1, 1] = a_s[b, 1, 1] - U[:128, :128]
        a_s[b, 1, 2] = a_s[b, 1, 2] - U[:128, 128:256]
        a_s[b, 2, 1] = a_s[b, 2, 1] - U[128:, :128]
        a_s[b, 2, 2] = a_s[b, 2, 2] - U[128:, 128:256]
        y_s[Y(b, 1)] = y_s[Y(b, 1)] - U[:128, 256:]
        y_s[Y(b, 2)] = y_s[Y(b, 2)] - U[128:, 256:]
        a_s[b, 0, 1] = R[:, :128]
        a_s[b, 0, 2] = R[:, 128:256]
        y_s[Y(b, 0)] = R[:, 256:]
    r = inverses([a_s[b, 1, 1] for b in range(NB)])
    for b in range(NB):
        R = mm3(r[b], jnp.concatenate([a_s[b, 1, 2], y_s[Y(b, 1)]], 1))
        U = mm3(jnp.concatenate([a_s[b, 0, 1], a_s[b, 2, 1]], 0), R)
        a_s[b, 0, 2] = a_s[b, 0, 2] - U[:128, :128]
        a_s[b, 1, 2] = R[:, :128]
        a_s[b, 2, 2] = a_s[b, 2, 2] - U[128:, :128]
        y_s[Y(b, 0)] = y_s[Y(b, 0)] - U[:128, 128:]
        y_s[Y(b, 1)] = R[:, 128:]
        y_s[Y(b, 2)] = y_s[Y(b, 2)] - U[128:, 128:]
    r = inverses([a_s[b, 2, 2] for b in range(NB)])
    torow = lambda m: jnp.sum(jnp.where(eye, m, 0.0), axis=0, keepdims=True)
    for b in range(NB):
        D = r[b]
        sw_s[b] = a_s[b, 2, 2]
        sr_s[b] = y_s[Y(b, 2)]
        ab = mm3(D, y_s[Y(b, 2)])
        G = jnp.concatenate([a_s[b, 0, 2], a_s[b, 1, 2]], 0)
        v = jnp.concatenate([y_s[Y(b, 0)], y_s[Y(b, 1)]], 0)
        Pa = mm3(G, jnp.concatenate([D, ab], 1))
        Pm = Pa[:, :128]
        ac = v - Pa[:, 128:]
        PT = mm3_t(D, G)
        Z = mm3_t(Pm, G)
        abr = torow(ab)
        acr = [torow(ac[:128]), torow(ac[128:])]
        vr = [torow(v[:128]), torow(v[128:])]
        acs = [ac[:128], ac[128:]]
        vs = [v[:128], v[128:]]
        rows = []
        for i in range(3):
            row = []
            for j in range(3):
                if i < 2 and j < 2:
                    gm = Z[128 * i:128 * i + 128, 128 * j:128 * j + 128] - acs[i] * acr[j] + vs[i] * vr[j]
                elif i < 2:
                    gm = -Pm[128 * i:128 * i + 128, :] - acs[i] * abr
                elif j < 2:
                    gm = -PT[:, 128 * j:128 * j + 128] - ab * acr[j]
                else:
                    gm = D - ab * abr
                t = 0.5 * gm * e_s[b, i, j]
                if i == j:
                    t = jnp.where(eye, 0.0, t)
                row.append(t)
            rows.append(jnp.concatenate(row, 1))
        eh, el = split(jnp.concatenate(rows, 0))
        F = f_s[pl.ds(384 * b, 384), :]
        Fo = jnp.concatenate([F, jnp.ones((384, 128), bf16)], 1)
        ef = mm(jnp.concatenate([eh, el], 1), jnp.concatenate([Fo, Fo], 0))
        cot_s[pl.ds(384 * b, 384), :] = ((-8.0 * weight / FEAT) * (ef[:, 128:] * F.astype(f32) - ef[:, :128])).astype(bf16)
    cot = cot_s[...]
    backed = mm_t(cot, wout16) * slope_s[...]
    gin = t_mm(x_s[...], backed.astype(bf16)).astype(bf16)
    gout = t_mm(cot, hid_s[...]).astype(bf16)
    gb = jnp.sum(backed, axis=0, keepdims=True).astype(bf16)
    gb8 = jnp.concatenate([gb[:, 128 * i:128 * i + 128] for i in range(4)] + [jnp.zeros((4, 128), bf16)], 0)
    for i in range(16):
        pk[i] = jnp.concatenate([gin[8 * i:8 * i + 8, :], gb8], 1)
        pk[16 + i] = jnp.concatenate([gout[8 * i:8 * i + 8, :], gb8], 1)

    plane = [(me + o) % 32 for o in range(1, 32)]
    for o, dev in enumerate(plane):
        push(pk.at[dev], rs_buf.at[me], rs_send.at[o], rs_recv.at[o], {"blk": dev})
    rs_buf[me] = pk[me]

    def sweep_groups(start, count):
        def step(i, carry):
            res = eliminate_group([sw_s[b] for b in range(NB)], [sr_s[b] for b in range(NB)])
            for b in range(NB):
                sw_s[b] = res[b][0]
                sr_s[b] = res[b][1]
                ww_s[b, start + i] = res[b][2]
            return carry
        lax.fori_loop(0, count, step, 0)

    sweep_groups(0, 3)
    for o in range(31):
        src = (me + 31 - o) % 32
        arrive(rs_buf.at[src], rs_send.at[o], rs_recv.at[o], {"blk": partner})
    acc = rs_buf[0].astype(f32)
    for i in range(1, 32):
        acc = acc + rs_buf[i].astype(f32)
    part[...] = acc.astype(bf16)
    z_buf[z] = acc.astype(bf16)
    for o, dev in enumerate(column):
        push(part, z_buf.at[z], z_send.at[o], z_recv.at[o], {"grp": dev})
    sweep_groups(3, 2)
    for o in range(7):
        src = (z + 7 - o) % 8
        arrive(z_buf.at[src], z_send.at[o], z_recv.at[o], {"blk": partner})
    acc = z_buf[0].astype(f32)
    for i in range(1, 8):
        acc = acc + z_buf[i].astype(f32)
    ag_buf[me] = acc[:, :512].astype(bf16)
    bias_out[...] = acc[:, 512:]
    for o, dev in enumerate(plane):
        push(ag_buf.at[me], ag_buf.at[me], ag_send.at[o], ag_recv.at[o], {"blk": dev})
    sweep_groups(5, 3)
    for b in range(NB):
        w_out[pl.ds(b, 1), :] = torow(jnp.concatenate([ww_s[b, g] for g in range(8)], 0))
    for o in range(31):
        src = (me + 31 - o) % 32
        arrive(ag_buf.at[src], ag_send.at[o], ag_recv.at[o], {"blk": partner})
    tot_out[...] = ag_buf[...]
    for cp in sends:
        cp.wait_send()


def main_call(nb, om, x, t, win, bin_, wout, weight):
    D = pltpu.SemaphoreType.DMA
    smem = pl.BlockSpec(memory_space=pltpu.SMEM)
    vmem = pl.BlockSpec(memory_space=V)
    return pl.pallas_call(
        functools.partial(main_kernel, weight),
        out_shape=(
            jax.ShapeDtypeStruct((2, 128), f32),
            jax.ShapeDtypeStruct((32, 8, 512), bf16),
            jax.ShapeDtypeStruct((8, 128), f32),
        ),
        in_specs=[smem, smem] + [vmem] * 5,
        out_specs=(vmem,) * 3,
        scratch_shapes=[
            V((16, 2, ROWS, 128), bf16), V((4, ROWS, 128), bf16), V((4, ROWS, 128), bf16),
            V((768, 128), bf16), V((768, 512), bf16), V((768, 512), f32), V((768, 128), bf16),
            V((2, 3, 3, 128, 128), f32), V((2, 3, 3, 128, 128), f32), V((6, 128, 128), f32), V((768, 128), bf16),
            V((2, 128, 128), f32), V((2, 128, 128), f32), V((2, 8, 16, 128), f32),
            V((32, 8, 640), bf16), V((32, 8, 640), bf16), V((8, 640), bf16), V((8, 8, 640), bf16), V((32, 8, 512), bf16),
            D((2, 15)), D((2, 15)), D((2,)), D((31,)), D((31,)), D((7,)), D((7,)), D((31,)), D((31,)),
        ],
        compiler_params=pltpu.CompilerParams(collective_id=0, has_side_effects=True),
        name="gradient_step",
    )(nb, om, x, t, win, bin_, wout)


def update_kernel(tot_ref, sum_ref, w_ref, win_ref, bin_ref, wout_ref, w_out, in_out, bias_out, out_out):
    bias = sum_ref[0:4, :]
    total = jnp.zeros((8, 512), f32)
    for i in range(32):
        t = tot_ref[i].astype(f32)
        total = total + t * t
    squares = jnp.sum(total) + jnp.sum(bias * bias)
    scale = 3.0 / jnp.sqrt(jnp.broadcast_to(squares, (1, 1)) + 1e-06)
    w_out[...] = w_ref[...]
    bias_out[...] = bin_ref[...] - scale * bias
    for i in range(16):
        in_out[pl.ds(8 * i, 8), :] = win_ref[pl.ds(8 * i, 8), :] - scale * tot_ref[i].astype(f32)
    for q in range(4):
        t = jnp.concatenate([tot_ref[16 + i][:, 128 * q:128 * q + 128].astype(f32) for i in range(16)], 0)
        out_out[pl.ds(128 * q, 128), :] = wout_ref[pl.ds(128 * q, 128), :] - scale * jnp.transpose(t)


def update_call(tot, total_bias, white, win, bias, wout):
    vmem = pl.BlockSpec(memory_space=V)
    return pl.pallas_call(
        update_kernel,
        out_shape=(
            jax.ShapeDtypeStruct((2, 128), f32),
            jax.ShapeDtypeStruct((128, 512), f32),
            jax.ShapeDtypeStruct((4, 128), f32),
            jax.ShapeDtypeStruct((512, 128), f32),
        ),
        in_specs=[vmem] * 6,
        out_specs=(vmem,) * 4,
        name="update_weights",
    )(tot, total_bias, white, win, bias, wout)


def shards(inputs, targets, weight_in, bias_in, weight_out, neighbors, owner_map):
    white, tot, total_bias = main_call(
        neighbors.T, owner_map, inputs, targets.reshape(2, PTS), weight_in, bias_in.reshape(1, -1), weight_out,
        1.0 / neighbors.shape[0],
    )
    white, new_in, new_bias, new_out = update_call(
        tot, total_bias, white, weight_in, bias_in.reshape(4, 128), weight_out
    )
    return (white.reshape(-1), new_in, new_bias.reshape(-1), new_out)


def solution(mesh):
    placed = (P(("grp", "blk"), None), P(("grp", "blk")), P(), P(), P(), P(), P())
    return jax.shard_map(
        shards,
        mesh=mesh,
        in_specs=placed,
        out_specs=(P(("grp", "blk")), P(), P(), P()),
        check_vma=False,
    )
```

time: 518 us -> 53.2 us (0.10)
  waiting for transfers between devices: 207 us -> 0 us
  other arithmetic: 161 us -> 0 us
  blocking collectives: 78.5 us -> 0 us
  Pallas kernels: 0 us -> 52.4 us
  starting transfers between devices: 18.9 us -> 0 us
  matrix products: 18.6 us -> 0 us
  between operations: 16.8 us -> 0.64 us
  local copies, waits for them, and re-layouts: 15.8 us -> 0 us
    psum x1 -> x0, waiting for transfers between devices: 174 us -> none  [apply_update(): lax.psum((gradients[0], gradients[1], gradients[2]), ('grp', 'blk'))]
    another operation x22 -> x0, other arithmetic: 152 us -> none  [the longest x8 66.9 us: block_terms(): chol_c = jnp.linalg.cholesky(exp_cc + nugget * eye_c)]
    psum x1 -> x0, blocking collectives: 78.5 us -> none  [apply_update(): lax.psum((gradients[0], gradients[1], gradients[2]), ('grp', 'blk'))]
    pallas_call x0 -> x2, Pallas kernels: none -> 52.4 us  [the longest x1 50.3 us: main_call(): pl.pallas_call(functools.partial(main_kernel, weight), out_shape=(jax.Sha...]
    all_to_all x3 -> x0, waiting for transfers between devices: 32.7 us -> none  [the longest x1 16.9 us: shards(): lax.all_to_all(back_rows, 'blk', split_axis=0, concat_axis=0, tiled=True)]
    all_to_all x3 -> x0, starting transfers between devices: 18.8 us -> none  [the longest x1 8.58 us: shards(): lax.all_to_all(send_targets, 'blk', split_axis=0, concat_axis=0, tiled=True)]
    dot_general x22 -> x0, matrix products: 13.5 us -> none  [the longest x1 2.03 us: features_of(): jnp.dot(rows_in, weight_in16, preferred_element_type=jnp.float32) + bias_now]
    another operation x11 -> x0, local copies, waits for them, and re-layouts: 5.5 us -> none
  transfers between devices with their start and end apart: 4 -> 0, of which waited for: 4 -> 0; matrix products, arithmetic and copies ran while one was open for 2% -> 0% of each run, Pallas kernels for 0% -> 0%
where the time goes in v2:
time: 53.2 us; the launch traced here: 53 us
  Pallas kernels  52.4 us (98%)
  between operations  0.64 us (1%)
    pallas_call x1, Pallas kernels, main_call(): pl.pallas_call(functools.partial(main_kernel, weight), out_shape=(jax.Sha...  50.3 us
    pallas_call x1, Pallas kernels, update_call(): pl.pallas_call(update_kernel, out_shape=(jax.ShapeDtypeStruct((2, 128), f...  2.12 us

profile of v2, /device:TPU:1, one launch (start us, length us, event | category | flops | bytes accessed | tf_op | source)
XLA Modules:
  0.0 53.0 jit_solution(4863856774432935338)
XLA Ops:
  0.6 50.3 %gradient_step.1 = (f32[2,128]{1,0:T(2,128)}, bf16[32,8,512]{2,1,0:T(8,128)(2,1)}, f32[8,128]{1,0:T(8,128)}) custom-call(s32[2,512]{1,0:T(2,128)} %bitcast.8, s32[512]{0:T(512)} %om_ref.1, bf16[256,128]{1,0:T(8,128)(2,1)} %x_ref.1, bf16[2,128]{1,0:T(2,128)(2,1)} %bitcast.9, f32[128,512]{1,0:T(8,128)} %win_ref.3, f32[1,512]{1,0:T(1,128)} %bitcast.6, ...), custom_call_target="tpu_custom_call" | custom-call | tf_op jit(solution)/shard_map/gradient_step/pallas_call | solution.py:364
  50.9 2.1 %update_weights.1 = (f32[2,128]{1,0:T(2,128)}, f32[128,512]{1,0:T(8,128)}, f32[4,128]{1,0:T(4,128)}, f32[512,128]{1,0:T(8,128)}) custom-call(bf16[32,8,512]{2,1,0:T(8,128)(2,1)} %get-tuple-element.11.tot_ref, f32[8,128]{1,0:T(8,128)} %get-tuple-element.12.sum_ref, f32[2,128]{1,0:T(2,128)} %get-tuple-element.13.w_ref, f32[128,512]{1,0:T(8,128)} %win_ref.3, ...), custom_call_target="tpu_custom_call" | custom-call | tf_op jit(solution)/shard_map/update_weights/pallas_call | solution.py:405

commit v3 on v2

--- a/solution.py
+++ b/solution.py
@@ -21,8 +21,9 @@
     return lax.dot_general(a,b,(((0,),(0,)),((),())),preferred_element_type=f32)
 
 def mm3(a,b):
-    ah,al=split(a); bh,bl=split(b)
-    return mm(jnp.concatenate([ah,al,ah],1),jnp.concatenate([bh,bh,bl],0))
+    ah,al=split(a); bh,bl=split(b); n=b.shape[1]
+    out=mm(jnp.concatenate([ah,al],1),jnp.concatenate([jnp.concatenate([bh,bl],1),jnp.concatenate([bh,jnp.zeros_like(bl)],1)],0))
+    return out[:,:n]+out[:,n:]
 
 def mm3_t(a,b):
     ah,al=split(a); bh,bl=split(b)
@@ -59,6 +60,7 @@
 
 
 MESH = pl.DeviceIdType.MESH
+MAIN_VMEM = 24 * 1024 * 1024
 V = pltpu.VMEM
 
 
@@ -104,9 +106,9 @@
 
 def main_kernel(weight, nb_ref, om_ref, x_ref, t_ref, win_ref, bin_ref, wout_ref,
                 w_out, tot_out, bias_out,
-                buf, give, take, x_s, hid_s, slope_s, f_s, e_s, a_s, y_s, cot_s, sw_s, sr_s, ww_s,
-                pk, rs_buf, part, z_buf, ag_buf,
-                g_send, g_recv, d_sem, rs_send, rs_recv, z_send, z_recv, ag_send, ag_recv):
+                nb_s, om_s, t_s, win_s, bin_s, wout_s, buf, give, take, x_s, hid_s, slope_s, f_s, e_s, a_s, y_s, cot_s, sw_s, sr_s, ww_s,
+                pk_a, pk_b, rs_a, rs_b, part_a, part_b, z_a, z_b,
+                in_sem, tokens, g_send, g_recv, d_sem, rs_send, rs_recv, z_send, z_recv, ag_send, ag_recv):
     me = lax.axis_index("blk")
     z = lax.axis_index("grp")
     here = (me // 8, (me // 2) % 4)
@@ -137,16 +139,31 @@
         ).wait_recv()
 
     barrier = pltpu.get_barrier_semaphore()
-    near = [{"blk": peer(f, d, 0)} for f in range(2) for d in (1, 2, 3)] + [{"blk": partner}]
-    column = [(z + o) % 8 for o in range(1, 8)]
-    greeted = near + [{"grp": d} for d in column]
-    for dev in greeted:
+    along = [{"grp": (z + d) % 8} for d in (1, 7)]
+    near = [{"blk": peer(f, d, 0)} for f in range(2) for d in (1, 2, 3)] + [{"blk": partner}] + along
+    for dev in near:
         pl.semaphore_signal(barrier, inc=1, device_id=dev, device_id_type=MESH)
-
+    fetches = []
+    for n, (src, dst) in enumerate((
+        (x_ref.at[pl.ds(0, 128)], buf.at[chip, 0, pl.ds(0, 128)]),
+        (x_ref.at[pl.ds(128, 128)], buf.at[chip, 1, pl.ds(0, 128)]),
+        (t_ref, t_s), (win_ref, win_s), (bin_ref, bin_s), (wout_ref, wout_s), (nb_ref, nb_s), (om_ref, om_s),
+    )):
+        cp = pltpu.make_async_copy(src, dst, in_sem.at[n])
+        cp.start()
+        fetches.append(cp)
+    for cp in fetches[:3]:
+        cp.wait()
     for h in range(2):
-        buf[chip, h, pl.ds(0, 128), :] = x_ref[pl.ds(128 * h, 128), :]
-        buf[chip, h, pl.ds(128, 8), :] = jnp.broadcast_to(t_ref[pl.ds(h, 1), :].astype(f32), (8, 128)).astype(bf16)
-    pl.semaphore_wait(barrier, len(greeted))
+        buf[chip, h, pl.ds(128, 8), :] = jnp.broadcast_to(t_s[pl.ds(h, 1), :].astype(f32), (8, 128)).astype(bf16)
+    pl.semaphore_wait(barrier, len(near))
+
+    def greet(n):
+        if n:
+            pl.semaphore_wait(tokens.at[n - 1], 2)
+        if n < 3:
+            for dev in along:
+                pl.semaphore_signal(tokens.at[n], inc=1, device_id=dev, device_id_type=MESH)
 
     def fan(h, at, axis, base):
         for n, d in ((2, 2), (0, 1), (1, 3)):
@@ -161,10 +178,13 @@
         fan(h, chip, firsts[h], 0)
     for h in range(2):
         fan(h, chip, 1 - firsts[h], 3)
-
-    win16 = win_ref[...].astype(bf16)
-    wout16 = wout_ref[...].astype(bf16)
-    bias = bin_ref[...]
+    greet(0)
+    for cp in fetches[3:]:
+        cp.wait()
+
+    win16 = win_s[...].astype(bf16)
+    wout16 = wout_s[...].astype(bf16)
+    bias = bin_s[...]
     eye = lax.broadcasted_iota(jnp.int32, (128, 128), 0) == lax.broadcasted_iota(jnp.int32, (128, 128), 1)
     ones = jnp.ones((128, 128), bf16)
 
@@ -189,16 +209,18 @@
             fan(h, at, 1 - firsts[h], 6 + 3 * n)
     for h in range(2):
         forward(3 * h + 2, buf[chip, h])
+    greet(1)
     for k in range(4):
         for n in (0, 1, 2):
             for h in range(2):
                 dp = 0 if k == 0 else origin[k - 1]
                 got(h, chip_at(firsts[h], dp, origin[n]), 3 + 3 * k + n)
 
+    greet(2)
     base = 64 * z
 
     def wanted(dev, n, j):
-        pos = om_ref[nb_ref[j, base + 2 * dev + n]] % 64
+        pos = om_s[nb_s[j, base + 2 * dev + n]] % 64
         return pos // 4, (pos // 2) % 2, pos % 2
 
     for n in range(2):
@@ -211,6 +233,7 @@
         for j in range(2):
             at, owner, half = wanted(me, n, j)
             mine.append((buf[at, half], owner))
+    greet(3)
     arrive(take, d_sem.at[0], d_sem.at[1], {"blk": partner})
     for n in range(2):
         for j in range(2):
@@ -300,19 +323,54 @@
         ef = mm(jnp.concatenate([eh, el], 1), jnp.concatenate([Fo, Fo], 0))
         cot_s[pl.ds(384 * b, 384), :] = ((-8.0 * weight / FEAT) * (ef[:, 128:] * F.astype(f32) - ef[:, :128])).astype(bf16)
     cot = cot_s[...]
+    steps = sorted(
+        ((dy, dx, dc) for dy in range(4) for dx in range(4) for dc in range(2) if (dy, dx, dc) != (0, 0, 0)),
+        key=lambda t: -(min(t[0], 4 - t[0]) + min(t[1], 4 - t[1])),
+    )
+    shifted = lambda dy, dx, dc: ((here[0] + dy) % 4) * 8 + ((here[1] + dx) % 4) * 2 + (core + dc) % 2
+    to = [shifted(*t) for t in steps]
+    back = [shifted(4 - t[0], 4 - t[1], t[2]) for t in steps]
+    updown = [4, 3, 5, 2, 6, 1, 7]
+    tile = lambda m, i: m[8 * (i // 2):8 * (i // 2) + 8, 256 * (i % 2):256 * (i % 2) + 256]
+
+    def scatter(k, pk, rs):
+        for o, dev in enumerate(to):
+            push(pk.at[dev], rs.at[me], rs_send.at[k, o], rs_recv.at[k, o], {"blk": dev})
+        rs[me] = pk[me]
+
+    def exchange(k, rs, part, zs):
+        for o, src in enumerate(back):
+            arrive(rs.at[src], rs_send.at[k, o], rs_recv.at[k, o], {"blk": partner})
+        acc = rs[0].astype(f32)
+        for i in range(1, 32):
+            acc = acc + rs[i].astype(f32)
+        part[...] = acc.astype(bf16)
+        zs[z] = acc.astype(bf16)
+        for o, d in enumerate(updown):
+            push(part, zs.at[z], z_send.at[k, o], z_recv.at[k, o], {"grp": (z + d) % 8})
+
+    def spread_sum(k, part, zs):
+        for o, d in enumerate(updown):
+            arrive(zs.at[(z + 8 - d) % 8], z_send.at[k, o], z_recv.at[k, o], {"blk": partner})
+        acc = zs[0].astype(f32)
+        for i in range(1, 8):
+            acc = acc + zs[i].astype(f32)
+        tot_out[k, me] = acc[:, :256].astype(bf16)
+        for o, dev in enumerate(to):
+            push(tot_out.at[k, me], tot_out.at[k, me], ag_send.at[k, o], ag_recv.at[k, o], {"blk": dev})
+        return acc
+
+    gout = t_mm(cot, hid_s[...]).astype(bf16)
+    for i in range(32):
+        pk_a[i] = tile(gout, i)
+    scatter(0, pk_a, rs_a)
     backed = mm_t(cot, wout16) * slope_s[...]
     gin = t_mm(x_s[...], backed.astype(bf16)).astype(bf16)
-    gout = t_mm(cot, hid_s[...]).astype(bf16)
     gb = jnp.sum(backed, axis=0, keepdims=True).astype(bf16)
     gb8 = jnp.concatenate([gb[:, 128 * i:128 * i + 128] for i in range(4)] + [jnp.zeros((4, 128), bf16)], 0)
-    for i in range(16):
-        pk[i] = jnp.concatenate([gin[8 * i:8 * i + 8, :], gb8], 1)
-        pk[16 + i] = jnp.concatenate([gout[8 * i:8 * i + 8, :], gb8], 1)
-
-    plane = [(me + o) % 32 for o in range(1, 32)]
-    for o, dev in enumerate(plane):
-        push(pk.at[dev], rs_buf.at[me], rs_send.at[o], rs_recv.at[o], {"blk": dev})
-    rs_buf[me] = pk[me]
+    for i in range(32):
+        pk_b[i] = jnp.concatenate([tile(gin, i), gb8], 1)
+    scatter(1, pk_b, rs_b)
 
     def sweep_groups(start, count):
         def step(i, carry):
@@ -325,82 +383,74 @@
         lax.fori_loop(0, count, step, 0)
 
     sweep_groups(0, 3)
-    for o in range(31):
-        src = (me + 31 - o) % 32
-        arrive(rs_buf.at[src], rs_send.at[o], rs_recv.at[o], {"blk": partner})
-    acc = rs_buf[0].astype(f32)
-    for i in range(1, 32):
-        acc = acc + rs_buf[i].astype(f32)
-    part[...] = acc.astype(bf16)
-    z_buf[z] = acc.astype(bf16)
-    for o, dev in enumerate(column):
-        push(part, z_buf.at[z], z_send.at[o], z_recv.at[o], {"grp": dev})
+    exchange(0, rs_a, part_a, z_a)
+    exchange(1, rs_b, part_b, z_b)
     sweep_groups(3, 2)
-    for o in range(7):
-        src = (z + 7 - o) % 8
-        arrive(z_buf.at[src], z_send.at[o], z_recv.at[o], {"blk": partner})
-    acc = z_buf[0].astype(f32)
-    for i in range(1, 8):
-        acc = acc + z_buf[i].astype(f32)
-    ag_buf[me] = acc[:, :512].astype(bf16)
-    bias_out[...] = acc[:, 512:]
-    for o, dev in enumerate(plane):
-        push(ag_buf.at[me], ag_buf.at[me], ag_send.at[o], ag_recv.at[o], {"blk": dev})
+    spread_sum(0, part_a, z_a)
+    bias_out[pl.ds(0, 4), :] = spread_sum(1, part_b, z_b)[:4, 256:]
+    for i in range(4):
+        bias_out[pl.ds(4 + i, 1), :] = bias[:, 128 * i:128 * i + 128]
     sweep_groups(5, 3)
     for b in range(NB):
         w_out[pl.ds(b, 1), :] = torow(jnp.concatenate([ww_s[b, g] for g in range(8)], 0))
-    for o in range(31):
-        src = (me + 31 - o) % 32
-        arrive(ag_buf.at[src], ag_send.at[o], ag_recv.at[o], {"blk": partner})
-    tot_out[...] = ag_buf[...]
+    for k in range(2):
+        for o, src in enumerate(back):
+            arrive(tot_out.at[k, src], ag_send.at[k, o], ag_recv.at[k, o], {"blk": partner})
     for cp in sends:
         cp.wait_send()
 
 
 def main_call(nb, om, x, t, win, bin_, wout, weight):
     D = pltpu.SemaphoreType.DMA
-    smem = pl.BlockSpec(memory_space=pltpu.SMEM)
+    any_ = pl.BlockSpec(memory_space=pltpu.HBM)
     vmem = pl.BlockSpec(memory_space=V)
     return pl.pallas_call(
         functools.partial(main_kernel, weight),
         out_shape=(
             jax.ShapeDtypeStruct((2, 128), f32),
-            jax.ShapeDtypeStruct((32, 8, 512), bf16),
+            jax.ShapeDtypeStruct((2, 32, 8, 256), bf16),
             jax.ShapeDtypeStruct((8, 128), f32),
         ),
-        in_specs=[smem, smem] + [vmem] * 5,
+        in_specs=[any_] * 7,
         out_specs=(vmem,) * 3,
         scratch_shapes=[
+            pltpu.SMEM(nb.shape, jnp.int32), pltpu.SMEM(om.shape, jnp.int32), V(t.shape, bf16),
+            V(win.shape, f32), V(bin_.shape, f32), V(wout.shape, f32),
             V((16, 2, ROWS, 128), bf16), V((4, ROWS, 128), bf16), V((4, ROWS, 128), bf16),
             V((768, 128), bf16), V((768, 512), bf16), V((768, 512), f32), V((768, 128), bf16),
             V((2, 3, 3, 128, 128), f32), V((2, 3, 3, 128, 128), f32), V((6, 128, 128), f32), V((768, 128), bf16),
             V((2, 128, 128), f32), V((2, 128, 128), f32), V((2, 8, 16, 128), f32),
-            V((32, 8, 640), bf16), V((32, 8, 640), bf16), V((8, 640), bf16), V((8, 8, 640), bf16), V((32, 8, 512), bf16),
-            D((2, 15)), D((2, 15)), D((2,)), D((31,)), D((31,)), D((7,)), D((7,)), D((31,)), D((31,)),
+            V((32, 8, 256), bf16), V((32, 8, 384), bf16), V((32, 8, 256), bf16), V((32, 8, 384), bf16),
+            V((8, 256), bf16), V((8, 384), bf16), V((8, 8, 256), bf16), V((8, 8, 384), bf16),
+            D((8,)), pltpu.SemaphoreType.REGULAR((3,)),
+            D((2, 15)), D((2, 15)), D((2,)), D((2, 31)), D((2, 31)), D((2, 7)), D((2, 7)), D((2, 31)), D((2, 31)),
         ],
-        compiler_params=pltpu.CompilerParams(collective_id=0, has_side_effects=True),
+        compiler_params=pltpu.CompilerParams(collective_id=0, has_side_effects=True, vmem_limit_bytes=MAIN_VMEM),
         name="gradient_step",
-    )(nb, om, x, t, win, bin_, wout)
-
-
-def update_kernel(tot_ref, sum_ref, w_ref, win_ref, bin_ref, wout_ref, w_out, in_out, bias_out, out_out):
+    )(*(pltpu.with_memory_space_constraint(v, pltpu.HBM) for v in (nb, om, x, t, win, bin_, wout)))
+
+
+def update_kernel(tot_ref, sum_ref, w_ref, win_ref, wout_ref, w_out, in_out, bias_out, out_out):
     bias = sum_ref[0:4, :]
-    total = jnp.zeros((8, 512), f32)
-    for i in range(32):
-        t = tot_ref[i].astype(f32)
-        total = total + t * t
+    total = jnp.zeros((8, 256), f32)
+    for k in range(2):
+        for i in range(32):
+            t = tot_ref[k, i].astype(f32)
+            total = total + t * t
     squares = jnp.sum(total) + jnp.sum(bias * bias)
     scale = 3.0 / jnp.sqrt(jnp.broadcast_to(squares, (1, 1)) + 1e-06)
     w_out[...] = w_ref[...]
-    bias_out[...] = bin_ref[...] - scale * bias
-    for i in range(16):
-        in_out[pl.ds(8 * i, 8), :] = win_ref[pl.ds(8 * i, 8), :] - scale * tot_ref[i].astype(f32)
+    bias_out[...] = sum_ref[4:8, :] - scale * bias
+    for i in range(32):
+        rows, lanes = pl.ds(8 * (i // 2), 8), pl.ds(256 * (i % 2), 256)
+        in_out[rows, lanes] = win_ref[rows, lanes] - scale * tot_ref[1, i].astype(f32)
     for q in range(4):
-        t = jnp.concatenate([tot_ref[16 + i][:, 128 * q:128 * q + 128].astype(f32) for i in range(16)], 0)
+        half, at = q // 2, 128 * (q % 2)
+        t = jnp.concatenate([tot_ref[0, 2 * i + half][:, at:at + 128].astype(f32) for i in range(16)], 0)
         out_out[pl.ds(128 * q, 128), :] = wout_ref[pl.ds(128 * q, 128), :] - scale * jnp.transpose(t)
 
 
-def update_call(tot, total_bias, white, win, bias, wout):
+def update_call(tot, total_bias, white, win, wout):
     vmem = pl.BlockSpec(memory_space=V)
     return pl.pallas_call(
         update_kernel,
@@ -410,10 +460,11 @@
             jax.ShapeDtypeStruct((4, 128), f32),
             jax.ShapeDtypeStruct((512, 128), f32),
         ),
-        in_specs=[vmem] * 6,
+        in_specs=[vmem] * 5,
         out_specs=(vmem,) * 4,
+        compiler_params=pltpu.CompilerParams(vmem_limit_bytes=8 * 1024 * 1024),
         name="update_weights",
-    )(tot, total_bias, white, win, bias, wout)
+    )(tot, total_bias, white, win, wout)
 
 
 def shards(inputs, targets, weight_in, bias_in, weight_out, neighbors, owner_map):
@@ -422,7 +473,7 @@
         1.0 / neighbors.shape[0],
     )
     white, new_in, new_bias, new_out = update_call(
-        tot, total_bias, white, weight_in, bias_in.reshape(4, 128), weight_out
+        tot, total_bias, white, weight_in, weight_out
     )
     return (white.reshape(-1), new_in, new_bias.reshape(-1), new_out)
 

time: 53.2 us -> 50.3 us (0.945)
  Pallas kernels: 52.4 us -> 49.6 us
    pallas_call x1, Pallas kernels: 50.3 us -> 48.6 us  [main_call(): pl.pallas_call(functools.partial(main_kernel, weight), out_shape=(jax.Sha...]
    pallas_call x1, Pallas kernels: 2.12 us -> 1 us  [update_call(): pl.pallas_call(update_kernel, out_shape=(jax.ShapeDtypeStruct((2, 128), f...]
where the time goes in v3:
time: 50.3 us; the launch traced here: 50.2 us
  Pallas kernels  49.6 us (99%)
  between operations  0.67 us (1%)
    pallas_call x1, Pallas kernels, main_call(): pl.pallas_call(functools.partial(main_kernel, weight), out_shape=(jax.Sha...  48.6 us

profile of v3, /device:TPU:1, one launch (start us, length us, event | category | flops | bytes accessed | tf_op | source)
XLA Modules:
  0.0 50.2 jit_solution(8525947988608431657)
XLA Ops:
  0.6 0.0 copy-start
  0.6 0.0 copy-start.1
  0.7 48.6 %gradient_step.1 = (f32[2,128]{1,0:T(2,128)S(1)}, bf16[2,32,8,256]{3,2,1,0:T(8,128)(2,1)S(1)}, f32[8,128]{1,0:T(8,128)S(1)}) custom-call(s32[2,512]{1,0:T(2,128)} %bitcast.5, s32[512]{0:T(512)} %om_ref.1, bf16[256,128]{1,0:T(8,128)(2,1)} %x_ref.1, bf16[2,128]{1,0:T(2,128)(2,1)} %bitcast.7, f32[128,512]{1,0:T(8,128)} %win_ref.3, f32[1,512]{1,0:T(1,128)} %bitcast.6, ...), custom_call_target="tpu_custom_call" | custom-call | tf_op jit(solution)/shard_map/gradient_step/pallas_call | solution.py:407
  49.2 0.0 copy-done
  49.2 0.0 copy-done.1
  49.2 1.0 %update_weights.1 = (f32[2,128]{1,0:T(2,128)}, f32[128,512]{1,0:T(8,128)}, f32[4,128]{1,0:T(4,128)}, f32[512,128]{1,0:T(8,128)}) custom-call(bf16[2,32,8,256]{3,2,1,0:T(8,128)(2,1)S(1)} %get-tuple-element.11.tot_ref, f32[8,128]{1,0:T(8,128)S(1)} %get-tuple-element.12.sum_ref, f32[2,128]{1,0:T(2,128)S(1)} %get-tuple-element.13.w_ref, f32[128,512]{1,0:T(8,128)S(1)} %copy-done, ...), custom_call_target="tpu_custom_call" | custom-call | tf_op jit(solution)/shard_map/update_weights/pallas_call | solution.py:455
Async XLA Ops:
  0.6 48.6 %copy-start = (f32[128,512]{1,0:T(8,128)S(1)}, f32[128,512]{1,0:T(8,128)}, u32[]{:S(2)}) copy-start(f32[128,512]{1,0:T(8,128)} %win_ref.3) | copy-start | bytes 786436
  0.6 48.6 %copy-start.1 = (f32[512,128]{1,0:T(8,128)S(1)}, f32[512,128]{1,0:T(8,128)}, u32[]{:S(2)}) copy-start(f32[512,128]{1,0:T(8,128)} %wout_ref.3) | copy-start | bytes 786436
